TPU v7x, 32 devices: a whole 2x2x4 slice. The times are simulated.
32 devices in a mesh: seg: 8 (over z, x), bank: 4 (over y, core).
Axes of the slice: x: 2, y: 2, z: 4, core: 2. Of those that a mesh axis runs over, the one named last changes fastest.
Arguments:
- strain: float32 [393216], P('seg'), may hold values from -24000 to 24000, as said below
- inv_asd: float32 [32768], replicated, may hold values from 0.3 to 3
- templates: bfloat16 [2, 8, 32768], P(None, 'bank'), may hold values from -6 to 6
- tmpl_len: int32 [8], P('bank'), may hold values from 2048 to 16384, as said below
- weights: float32 [8], P('bank'), may hold values from 0.2 to 5
- chirp_mass: float32 [8], P('bank'), may hold values from 10 to 60
- valid: int32 [384], P('seg'), may hold values 0 or 1
Outputs:
- log_like: float32 [393216], P(('seg', 'bank'))
- chirp_mean: float32 [393216], P(('seg', 'bank'))
- delay_mean: float32 [393216], P(('seg', 'bank'))
Inputs may be any that keep to these rules, and one draw needn't show every extreme that they name: `strain`: noise amplitude may change from one block of 1024 samples to the next. `tmpl_len`: template lengths lie between 2048 and 16384 samples, both ends taken.
All inputs are finite; a program needn't handle non-finite values. No bound on the sum of `valid` on one device may be relied on, other than what follows from the above.
Results may differ from a plain program's by a relative error of at most 0.00035.
Values sent between devices are 32-bit elements; how exact they have to be, the bound alone decides.
No kernel may reach another device: no remote copies, remote signals or barrier semaphores. Data moves between devices by JAX's collectives and lax.ppermute only.
A program may use at most 64 MiB of HBM per device.

v0:
```python
import math

import jax
import jax.numpy as jnp
from jax import lax
from jax.sharding import PartitionSpec as P

NFFT = 65536
FA = 256
OVER = 16384
RATE = 4096
HOP = 49152


HIGH = lax.Precision.HIGHEST


def passed_along(array, axis, by):
    length = lax.axis_size(axis)
    pairs = [(i, i + by) for i in range(length) if 0 <= i + by < length]
    return lax.ppermute(array, axis, pairs)


def log_bessel(rho_val):
    small_x = jnp.minimum(rho_val, 3.75)
    small_t = (small_x / 3.75) ** 2
    small_poly = 1.0 + small_t * (
        3.5156229
        + small_t
        * (
            3.0899424
            + small_t
            * (1.2067492 + small_t * (0.2659732 + small_t * (0.0360768 + small_t * 0.0045813)))
        )
    )
    large_x = jnp.maximum(rho_val, 3.75)
    large_q = 3.75 / large_x
    large_poly = 0.39894228 + large_q * (
        0.01328592
        + large_q
        * (
            0.00225319
            + large_q
            * (
                -0.00157565
                + large_q
                * (
                    0.00916281
                    + large_q
                    * (
                        -0.02057706
                        + large_q * (0.02635537 + large_q * (-0.01647633 + large_q * 0.00392377))
                    )
                )
            )
        )
    )
    large_val = large_x - 0.5 * jnp.log(large_x) + jnp.log(large_poly)
    return jnp.where(rho_val < 3.75, jnp.log(small_poly), large_val)


def phase_table(row_count, col_count, period):
    index_grid = (
        jnp.arange(row_count, dtype=jnp.int32)[:, None]
        * jnp.arange(col_count, dtype=jnp.int32)[None, :]
        % period
    )
    angles = index_grid.astype(jnp.float32) * (2.0 * math.pi / period)
    return (jnp.cos(angles), jnp.sin(angles))


def contract_last(left_mat, right_mat):
    return lax.dot_general(
        left_mat,
        right_mat,
        (((1,), (1,)), ((), ())),
        precision=HIGH,
        preferred_element_type=jnp.float32,
    )


def pick_row(score_row, begin_at):
    return lax.dynamic_slice_in_dim(score_row, begin_at, HOP)


def finish(peak_score, total, chirp_sum, delay_sum, prior_sum):
    return (peak_score + jnp.log(total) - jnp.log(prior_sum), chirp_sum / total, delay_sum / total)


def local(strain, inv_asd, templates, tmpl_len, weights, chirp_mass, valid):
    hop_len = strain.shape[0]
    block_count = valid.shape[0]
    fb_len = NFFT // FA
    half_rows = fb_len // 2
    local_count = templates.shape[1]
    gated_data = (
        strain.reshape(block_count, hop_len // block_count) * valid.astype(jnp.float32)[:, None]
    ).reshape(hop_len)
    earlier = passed_along(gated_data[hop_len - OVER :], "seg", 1)
    window = jnp.concatenate([earlier, gated_data])
    frame_rows = window.reshape(FA, fb_len)
    short_cos, short_sin = phase_table(FA, FA, FA)
    twist_cos, twist_sin = phase_table(FA, fb_len, NFFT)
    long_cos, long_sin = phase_table(half_rows, fb_len, fb_len)
    section_re = jnp.dot(short_cos, frame_rows, precision=HIGH, preferred_element_type=jnp.float32)
    section_im = -jnp.dot(short_sin, frame_rows, precision=HIGH, preferred_element_type=jnp.float32)
    turned_re = section_re * twist_cos + section_im * twist_sin
    turned_im = section_im * twist_cos - section_re * twist_sin
    bin_scale = inv_asd.reshape(half_rows, FA) / math.sqrt(NFFT)
    spec_re = (contract_last(long_cos, turned_re) + contract_last(long_sin, turned_im)) * bin_scale
    spec_im = (contract_last(long_cos, turned_im) - contract_last(long_sin, turned_re)) * bin_scale
    tmpl_re = templates[0].astype(jnp.float32).reshape(local_count, half_rows, FA)
    tmpl_im = templates[1].astype(jnp.float32).reshape(local_count, half_rows, FA)
    asd_sq = (inv_asd * inv_asd).reshape(half_rows, FA)
    sigma_sq = jnp.sum(asd_sq[None] * (tmpl_re * tmpl_re + tmpl_im * tmpl_im), axis=(1, 2))
    prod_re = spec_re[None] * tmpl_re + spec_im[None] * tmpl_im
    prod_im = spec_im[None] * tmpl_re - spec_re[None] * tmpl_im
    inner_re = jnp.einsum("kab,ac->kbc", prod_re, long_cos, precision=HIGH) - jnp.einsum(
        "kab,ac->kbc", prod_im, long_sin, precision=HIGH
    )
    inner_im = jnp.einsum("kab,ac->kbc", prod_re, long_sin, precision=HIGH) + jnp.einsum(
        "kab,ac->kbc", prod_im, long_cos, precision=HIGH
    )
    twisted_re = inner_re * twist_cos[None] - inner_im * twist_sin[None]
    twisted_im = inner_re * twist_sin[None] + inner_im * twist_cos[None]
    corr_re = (
        jnp.einsum("tb,kbc->ktc", short_cos, twisted_re, precision=HIGH)
        - jnp.einsum("tb,kbc->ktc", short_sin, twisted_im, precision=HIGH)
    ).reshape(local_count, NFFT)
    corr_im = (
        jnp.einsum("tb,kbc->ktc", short_cos, twisted_im, precision=HIGH)
        + jnp.einsum("tb,kbc->ktc", short_sin, twisted_re, precision=HIGH)
    ).reshape(local_count, NFFT)
    rho_val = jnp.sqrt((corr_re * corr_re + corr_im * corr_im) / sigma_sq[:, None])
    scores = log_bessel(rho_val)
    starts = OVER - tmpl_len
    aligned = jax.vmap(pick_row)(scores, starts)
    delays = tmpl_len.astype(jnp.float32) / RATE
    bank_count = lax.axis_size("bank")
    traits = jnp.stack([weights, chirp_mass, delays], axis=1)
    traits_rep = jnp.tile(traits, (1, bank_count))
    bank_scores, bank_traits = (
        lax.all_to_all(aligned, "bank", split_axis=1, concat_axis=0, tiled=True),
        lax.all_to_all(traits_rep, "bank", split_axis=1, concat_axis=0, tiled=True),
    )
    all_weights = bank_traits[:, 0]
    peak_score = jnp.max(bank_scores, axis=0)
    masses = all_weights[:, None] * jnp.exp(bank_scores - peak_score[None, :])
    total = jnp.sum(masses, axis=0)
    chirp_sum = jnp.sum(masses * bank_traits[:, 1][:, None], axis=0)
    delay_sum = jnp.sum(masses * bank_traits[:, 2][:, None], axis=0)
    return finish(peak_score, total, chirp_sum, delay_sum, jnp.sum(all_weights))


def solution(mesh):
    placed = (P("seg"), P(), P(None, "bank", None), P("bank"), P("bank"), P("bank"), P("seg"))
    return jax.shard_map(
        local,
        mesh=mesh,
        in_specs=placed,
        out_specs=(P(("seg", "bank")), P(("seg", "bank")), P(("seg", "bank"))),
        check_vma=False,
    )
```

profile of v0, /device:TPU:0, one launch (start us, length us, event | category | flops | bytes accessed | tf_op | source)
XLA Modules:
  0.0 70.7 jit_solution(14591296255125556895)
XLA Ops:
  1.4 1.0 %reshape.124 = f32[48,1024]{1,0:T(8,128)S(1)} reshape(f32[49152]{0:T(1024)} %param.7) | data formatting | bytes 393216 | tf_op jit(solution)/shard_map/reshape | solution.py:97
  2.4 4.9 %collective-permute-start = (f32[16384]{0:T(1024)S(1)}, f32[16384]{0:T(1024)S(1)}, u32[]{:S(2)}, u32[]{:S(2)}) collective-permute-start(f32[16384]{0:T(1024)S(1)} %bitcast.74), channel_id=1, source_target_pairs={{0,4},{4,8},{8,12},{12,16},{16,20},{20,24},{24,28},{1,5},{5,9},{9,... | collective-permute-start | bytes 196616 | tf_op jit(solution)/shard_map/ppermute | solution.py:21
  8.7 3.2 %all-to-all-start.1 = ((f32[2,4,3]{2,0,1:T(2,128)}), f32[2,4,3]{2,0,1:T(2,128)S(1)}, u32[]{:S(2)}, u32[]{:S(2)}) async-start(f32[2,4,3]{2,0,1:T(2,128)} %tile.2), calls=%async_computation.1 | async-start | bytes 8192 | tf_op jit(solution)/shard_map/all_to_all | solution.py:144
  12.1 0.9 %copy-done.1 = f32[49152]{0:T(1024)S(1)} copy-done((f32[49152]{0:T(1024)S(1)}, f32[49152]{0:T(1024)}, u32[]{:S(2)}) %copy-start.1) | copy-done | bytes 196632
  13.0 0.9 %copy-done.2 = f32[32768]{0:T(1024)S(1)} copy-done((f32[32768]{0:T(1024)S(1)}, f32[32768]{0:T(1024)}, u32[]{:S(2)}) %copy-start.2) | copy-done | bytes 131096
  14.0 0.9 %copy-done = bf16[2,2,32768]{2,1,0:T(2,128)(2,1)S(1)} copy-done((bf16[2,2,32768]{2,1,0:T(2,128)(2,1)S(1)}, bf16[2,2,32768]{2,1,0:T(2,128)(2,1)}, u32[]{:S(2)}) %copy-start) | copy-done | bytes 262168
  15.9 1.0 %fusion.33 = (f32[256,256]{1,0:T(8,128)S(1)}, f32[256,256]{1,0:T(8,128)S(1)}) fusion(), kind=kLoop, calls=%fused_computation.67 | loop fusion | flops 917504 | bytes 524288 | tf_op jit(solution)/shard_map/sin | solution.py:69
  17.0 1.6 %convolution_negate_fusion = f32[256,256]{1,0:T(8,128)S(1)} fusion(f32[256,256]{1,0:T(8,128)S(1)} %reshape.125), kind=kOutput, calls=%fused_computation.9 | convolution fusion | flops 202309632 | bytes 524288 | tf_op jit(solution)/shard_map/dot_general | solution.py:106
  18.7 1.8 %fusion.39 = f32[256,256]{1,0:T(8,128)S(1)} fusion(f32[256,256]{1,0:T(8,128)S(1)} %reshape.125), kind=kOutput, calls=%fused_computation.71 | convolution fusion | flops 202244096 | bytes 524288 | tf_op jit(solution)/shard_map/dot_general | solution.py:105
  20.5 1.9 %fusion.54 = f32[128,256]{1,0:T(8,128)S(1)} fusion(f32[256,256]{1,0:T(8,128)S(1)} %convolution_negate_fusion, f32[256,256]{1,0:T(8,128)S(1)} %fusion.39), kind=kOutput, calls=%fused_computation.82 | convolution fusion | flops 102236160 | bytes 655360 | tf_op jit(solution)/shard_map/dot_general | solution.py:73
  22.3 1.9 %fusion.52 = f32[128,256]{1,0:T(8,128)S(1)} fusion(f32[256,256]{1,0:T(8,128)S(1)} %fusion.39, f32[256,256]{1,0:T(8,128)S(1)} %convolution_negate_fusion), kind=kOutput, calls=%fused_computation.81 | convolution fusion | flops 102236160 | bytes 655360 | tf_op jit(solution)/shard_map/dot_general | solution.py:73
  24.2 1.9 %fusion.5 = f32[128,256]{1,0:T(8,128)S(1)} fusion(f32[128,256]{1,0:T(8,128)S(1)} %div.33, f32[128,256]{1,0:T(8,128)S(1)} %fusion.54, f32[256,256]{1,0:T(8,128)S(1)} %fusion.39, f32[256,256]{1,0:T(8,128)S(1)} %convolution_negate_fusion), kind=kOutput, calls=%fused_computation.13 | convolution fusion | flops 102301696 | bytes 917504 | tf_op jit(solution)/shard_map/dot_general | solution.py:73
  26.2 1.9 %fusion.4 = f32[128,256]{1,0:T(8,128)S(1)} fusion(f32[128,256]{1,0:T(8,128)S(1)} %div.33, f32[128,256]{1,0:T(8,128)S(1)} %fusion.52, f32[256,256]{1,0:T(8,128)S(1)} %convolution_negate_fusion, f32[256,256]{1,0:T(8,128)S(1)} %fusion.39), kind=kOutput, calls=%fused_computation.11 | convolution fusion | flops 102301696 | bytes 917504 | tf_op jit(solution)/shard_map/dot_general | solution.py:73
  28.2 1.1 %fusion.31 = f32[2,256,256]{2,1,0:T(8,128)S(1)} fusion(f32[2,128,256]{1,2,0:T(8,128)S(1)} %copy.44, f32[2,128,256]{1,2,0:T(8,128)S(1)} %copy.42, f32[128,256]{0,1:T(8,128)S(1)} %copy.43, f32[128,256]{0,1:T(8,128)S(1)} %copy.41), kind=kOutput, calls=%fused_computation.63 | convolution fusion | flops 201981952 | bytes 1310720 | tf_op jit(solution)/shard_map/kab,ac->kbc/dot_general | solution.py:118
  29.3 1.1 %fusion.27 = f32[2,256,256]{2,1,0:T(8,128)S(1)} fusion(f32[2,128,256]{1,2,0:T(8,128)S(1)} %copy.44, f32[2,128,256]{1,2,0:T(8,128)S(1)} %copy.42, f32[128,256]{0,1:T(8,128)S(1)} %copy.43, f32[128,256]{0,1:T(8,128)S(1)} %copy.41), kind=kOutput, calls=%fused_computation.59 | convolution fusion | flops 201981952 | bytes 1310720 | tf_op jit(solution)/shard_map/kab,ac->kbc/dot_general | solution.py:121
  30.3 1.1 %convolution_subtract_fusion = f32[2,256,256]{2,1,0:T(8,128)S(1)} fusion(f32[2,256,256]{2,1,0:T(8,128)S(1)} %fusion.31, f32[2,128,256]{1,2,0:T(8,128)S(1)} %copy.44, f32[2,128,256]{1,2,0:T(8,128)S(1)} %copy.42, f32[128,256]{0,1:T(8,128)S(1)} %copy.43, f32[128,256]{0,1:T(8,128)S(1)} %copy.41), kind=kOutput, calls=%fused_computation.2 | convolution fusion | flops 202113024 | bytes 1835008 | tf_op jit(solution)/shard_map/kab,ac->kbc/dot_general | solution.py:118
  31.4 1.1 %convolution_add_fusion = f32[2,256,256]{2,1,0:T(8,128)S(1)} fusion(f32[2,256,256]{2,1,0:T(8,128)S(1)} %fusion.27, f32[2,128,256]{1,2,0:T(8,128)S(1)} %copy.44, f32[2,128,256]{1,2,0:T(8,128)S(1)} %copy.42, f32[128,256]{0,1:T(8,128)S(1)} %copy.43, f32[128,256]{0,1:T(8,128)S(1)} %copy.41), kind=kOutput, calls=%fused_computation.1 | convolution fusion | flops 202113024 | bytes 1835008 | tf_op jit(solution)/shard_map/kab,ac->kbc/dot_general | solution.py:121
  32.5 2.1 %fusion.13 = f32[2,256,256]{2,1,0:T(8,128)S(1)} fusion(f32[2,256,256]{2,1,0:T(8,128)S(1)} %convolution_add_fusion, f32[2,256,256]{2,1,0:T(8,128)S(1)} %convolution_subtract_fusion, f32[256,256]{1,0:T(8,128)S(1)} %get-tuple-element.47, f32[256,256]{1,0:T(8,128)S(1)} %get-tuple-element.48), kind=kOutput, calls=%fused_computation.36 | convolution fusion | flops 403963904 | bytes 2097152 | tf_op jit(solution)/shard_map/tb,kbc->ktc/dot_general | solution.py:131
  34.6 1.9 %fusion.15 = f32[2,256,256]{2,1,0:T(8,128)S(1)} fusion(f32[2,256,256]{2,1,0:T(8,128)S(1)} %convolution_add_fusion, f32[2,256,256]{2,1,0:T(8,128)S(1)} %convolution_subtract_fusion, f32[256,256]{1,0:T(8,128)S(1)} %get-tuple-element.47, f32[256,256]{1,0:T(8,128)S(1)} %get-tuple-element.48), kind=kOutput, calls=%fused_computation.38 | convolution fusion | flops 403963904 | bytes 2097152 | tf_op jit(solution)/shard_map/tb,kbc->ktc/dot_general | solution.py:127
  36.4 1.9 %fusion.3 = f32[2,256,256]{2,1,0:T(8,128)S(1)} fusion(f32[2,256,256]{2,1,0:T(8,128)S(1)} %fusion.15, f32[2,256,256]{2,1,0:T(8,128)S(1)} %convolution_add_fusion, f32[2,256,256]{2,1,0:T(8,128)S(1)} %convolution_subtract_fusion, f32[256,256]{1,0:T(8,128)S(1)} %get-tuple-element.47, f32[256,256]{1,0:T(8,128)S(1)} %get-tuple-element.48), kind=kOutput, calls=%fused_computation.8 | convolution fusion | flops 404226048 | bytes 2621440 | tf_op jit(solution)/shard_map/tb,kbc->ktc/dot_general | solution.py:128
  38.3 1.9 %fusion.2 = f32[2,256,256]{1,2,0:T(8,128)S(1)} fusion(f32[2,256,256]{2,1,0:T(8,128)S(1)} %fusion.3, f32[2,256,256]{2,1,0:T(8,128)S(1)} %fusion.13, f32[2,256,256]{2,1,0:T(8,128)S(1)} %convolution_add_fusion, f32[2,256,256]{2,1,0:T(8,128)S(1)} %convolution_subtract_fusion, f32[256,256]{1,0:T(8,128)S(1)} %get-tuple-element.47, ...), kind=kOutput, calls=%fused_computation.6 | convolution fusion | flops 404357120 | bytes 3145728 | tf_op jit(solution)/shard_map/tb,kbc->ktc/dot_general | solution.py:132
  40.8 3.8 %compare_select_fusion = f32[2,65536]{1,0:T(2,128)S(1)} fusion(f32[2,65536]{1,0:T(2,128)S(1)} %bitcast.66, f32[2]{0:T(128)S(1)} %multiply_reduce_fusion.2), kind=kLoop, calls=%fused_computation.14 | loop fusion | flops 5111808 | bytes 1048584 | tf_op jit(solution)/shard_map/jit(_where)/select_n | solution.py:59
  44.6 13.4 %while.1 = (s32[]{:T(128)}, f32[2,65536]{1,0:T(2,128)S(1)}, s32[2,2]{1,0:T(2,128)S(1)}, f32[2,49152]{1,0:T(2,128)}, s32[]{:T(128)}, /*index=5*/s32[]{:T(128)}) while((s32[]{:T(128)}, f32[2,65536]{1,0:T(2,128)S(1)}, s32[2,2]{1,0:T(2,128)S(1)}, f32[2,49152]{1,0:T(2,128)}, s32[]{:T(128)}, /*index=5*/s32[]{:T(128)}) %tuple.36), condition=%wide.while_cond, body=%wide.while_body.sunk | while | flops 2 | bytes 786545 | solution.py:83
  45.3 1.7 %dynamic-slice.7 = f32[1,49152]{1,0:T(1,128)S(1)} dynamic-slice(f32[2,65536]{1,0:T(2,128)S(1)} %get-tuple-element.91, s32[]{:T(128)} %bitcast.64, s32[]{:T(128)} %bitcast.65), dynamic_slice_sizes={1,49152} | dynamic-slice | bytes 393220 | tf_op jit(solution)/shard_map/vmap()/gather
  47.0 4.4 %dynamic-update-slice.3 = f32[2,49152]{1,0:T(2,128)} dynamic-update-slice(f32[2,49152]{1,0:T(2,128)} %get-tuple-element.87, f32[1,49152]{1,0:T(1,128)S(1)} %dynamic-slice.7, s32[]{:T(128)} %get-tuple-element.84, s32[]{:T(128)} %constant.32.clone.1..sunk) | dynamic-update-slice | bytes 393220 | tf_op jit(solution)/shard_map/vmap()/gather
  52.0 1.7 %dynamic-slice.7 = f32[1,49152]{1,0:T(1,128)S(1)} dynamic-slice(f32[2,65536]{1,0:T(2,128)S(1)} %get-tuple-element.91, s32[]{:T(128)} %bitcast.64, s32[]{:T(128)} %bitcast.65), dynamic_slice_sizes={1,49152} | dynamic-slice | bytes 393220 | tf_op jit(solution)/shard_map/vmap()/gather
  53.7 4.4 %dynamic-update-slice.3 = f32[2,49152]{1,0:T(2,128)} dynamic-update-slice(f32[2,49152]{1,0:T(2,128)} %get-tuple-element.87, f32[1,49152]{1,0:T(1,128)S(1)} %dynamic-slice.7, s32[]{:T(128)} %get-tuple-element.84, s32[]{:T(128)} %constant.32.clone.1..sunk) | dynamic-update-slice | bytes 393220 | tf_op jit(solution)/shard_map/vmap()/gather
  58.1 3.5 %all-to-all-start = ((f32[2,4,12288]{2,0,1:T(2,128)}), f32[2,4,12288]{2,0,1:T(2,128)S(1)}, u32[]{:S(2)}, u32[]{:S(2)}) async-start(f32[2,4,12288]{2,0,1:T(2,128)} %bitcast.6), calls=%async_computation | async-start | bytes 786432 | tf_op jit(solution)/shard_map/all_to_all | solution.py:143
  61.6 0.7 slice_reduce_fusion
  63.2 5.8 %all-to-all-done = f32[2,4,12288]{2,0,1:T(2,128)S(1)} async-done(((f32[2,4,12288]{2,0,1:T(2,128)}), f32[2,4,12288]{2,0,1:T(2,128)S(1)}, u32[]{:S(2)}, u32[]{:S(2)}) %all-to-all-start) | async-done | bytes 393248 | tf_op jit(solution)/shard_map/all_to_all | solution.py:143
  69.1 0.9 %multiply_reduce_fusion = (f32[12288]{0:T(1024)S(1)}, f32[12288]{0:T(1024)S(1)}, f32[12288]{0:T(1024)S(1)}) fusion(f32[4,2]{1,0:T(4,128)S(1)} %mul.498, f32[2,4,12288]{2,0,1:T(2,128)S(1)} %all-to-all-done, f32[12288]{0:T(1024)S(1)} %reduce_max.9, f32[4,2]{1,0:T(4,128)S(1)} %mul.492, f32[4,2]{1,0:T(4,128)S(1)} %mul.495), kind=kLoop, calls=%fused_computation.20 | loop fusion | flops 651264 | bytes 589920 | tf_op jit(solution)/shard_map/reduce_sum | solution.py:151
  70.0 0.7 fusion.131
  (49 shorter events, 5.8 us)
Async XLA Ops:
  2.4 4.9 %copy-start.5 = (s32[2]{0:T(128)S(1)}, s32[2]{0:T(128)}, u32[]{:S(2)}) copy-start(s32[2]{0:T(128)} %param.10) | copy-start | bytes 28
  2.4 14.5 %collective-permute-start = (f32[16384]{0:T(1024)S(1)}, f32[16384]{0:T(1024)S(1)}, u32[]{:S(2)}, u32[]{:S(2)}) collective-permute-start(f32[16384]{0:T(1024)S(1)} %bitcast.74), channel_id=1, source_target_pairs={{0,4},{4,8},{8,12},{12,16},{16,20},{20,24},{24,28},{1,5},{5,9},{9,... | collective-permute-start | bytes 196616 | tf_op jit(solution)/shard_map/ppermute | solution.py:21
  7.3 0.7 copy-start.3
  7.4 0.7 copy-start.4
  8.7 49.4 %all-to-all-start.1 = ((f32[2,4,3]{2,0,1:T(2,128)}), f32[2,4,3]{2,0,1:T(2,128)S(1)}, u32[]{:S(2)}, u32[]{:S(2)}) async-start(f32[2,4,3]{2,0,1:T(2,128)} %tile.2), calls=%async_computation.1 | async-start | bytes 8192 | tf_op jit(solution)/shard_map/all_to_all | solution.py:144
  12.1 0.9 %copy-start.1 = (f32[49152]{0:T(1024)S(1)}, f32[49152]{0:T(1024)}, u32[]{:S(2)}) copy-start(f32[49152]{0:T(1024)} %param.7) | copy-start | bytes 589828
  13.0 0.9 %copy-start.2 = (f32[32768]{0:T(1024)S(1)}, f32[32768]{0:T(1024)}, u32[]{:S(2)}) copy-start(f32[32768]{0:T(1024)} %param.8) | copy-start | bytes 393220
  13.9 0.9 %copy-start = (bf16[2,2,32768]{2,1,0:T(2,128)(2,1)S(1)}, bf16[2,2,32768]{2,1,0:T(2,128)(2,1)}, u32[]{:S(2)}) copy-start(bf16[2,2,32768]{2,1,0:T(2,128)(2,1)} %param.9) | copy-start | bytes 786436
  58.1 10.8 %all-to-all-start = ((f32[2,4,12288]{2,0,1:T(2,128)}), f32[2,4,12288]{2,0,1:T(2,128)S(1)}, u32[]{:S(2)}, u32[]{:S(2)}) async-start(f32[2,4,12288]{2,0,1:T(2,128)} %bitcast.6), calls=%async_computation | async-start | bytes 786432 | tf_op jit(solution)/shard_map/all_to_all | solution.py:143
where the time goes:
time: 71.6 us; the launch traced here: 70.7 us
  matrix products  22.9 us (32%)
  local copies, waits for them, and re-layouts  20.1 us (28%)
  starting transfers between devices  11.6 us (16%)
  other arithmetic  8.63 us (12%)
  waiting for transfers between devices  5.77 us (8%)
  between operations  1.69 us (2%)
    gather x8, local copies, waits for them, and re-layouts  13.4 us
    dot_general x4, matrix products, contract_last(): lax.dot_general(left_mat, right_mat, (((1,), (1,)), ((), ())), precision=...  7.51 us
    all_to_all x1, waiting for transfers between devices, local(): lax.all_to_all(aligned, 'bank', split_axis=1, concat_axis=0, tiled=True)  5.76 us
    ppermute x1, starting transfers between devices, passed_along(): return lax.ppermute(array, axis, pairs)  4.87 us
    unnamed x20, local copies, waits for them, and re-layouts  3.98 us
    select_n x1, other arithmetic, log_bessel(): return jnp.where(rho_val < 3.75, jnp.log(small_poly), large_val)  3.79 us
    all_to_all x1, starting transfers between devices, local(): lax.all_to_all(aligned, 'bank', split_axis=1, concat_axis=0, tiled=True)  3.46 us
    all_to_all x1, starting transfers between devices, local(): lax.all_to_all(traits_rep, 'bank', split_axis=1, concat_axis=0, tiled=True)  3.25 us
  transfers between devices with their start and end apart: 3, of which 1 were waited for; matrix products, arithmetic and copies ran while one was open for 63% of the time, Pallas kernels for 0%

commit v1 on v0

v1 whole, which is shorter than its diff:
```python
import functools
import math

import jax
import jax.numpy as jnp
import numpy as np
from jax import lax
from jax.experimental import pallas as pl
from jax.experimental.pallas import tpu as pltpu
from jax.sharding import PartitionSpec as P

NFFT = 65536
FA = 256
HALF = 128
OVER = 16384
RATE = 4096
LANES = 128
F32 = jnp.float32
BF16 = jnp.bfloat16

TERMS = ((0, 0), (0, 1), (1, 0), (1, 1), (0, 2), (2, 0))
PARTS = 1 + max(max(term) for term in TERMS)


def parts_of_table(table):
    rest = np.asarray(table, np.float32)
    parts = []
    for _ in range(PARTS):
        part = rest.astype(jnp.bfloat16)
        parts.append(part)
        rest = rest - part.astype(np.float32)
    return parts


@functools.cache
def tables():
    index = np.arange(FA, dtype=np.int64)
    grid = index[:, None] * index[None, :]
    angle = (grid % FA) * (2.0 * math.pi / FA)
    cos_parts = parts_of_table(np.cos(angle))
    sin_parts = parts_of_table(np.sin(angle))
    neg_parts = [-part for part in sin_parts]
    fine = grid * (2.0 * math.pi / NFFT)
    twist = np.stack([np.cos(fine), np.sin(fine)]).astype(np.float32)
    rows = OVER // FA
    head = np.concatenate(
        [np.concatenate([cos_parts[i][:, :rows], neg_parts[i][:, :rows]]) for i, _ in TERMS], axis=1
    )
    return {
        "dft": np.stack([np.stack(cos_parts), np.stack(sin_parts), np.stack(neg_parts)]),
        "twist": twist,
        "head": head,
    }


def split(value):
    parts = []
    for step in range(PARTS):
        part = value.astype(BF16)
        parts.append(part)
        if step < PARTS - 1:
            value = value - part.astype(F32)
    return parts


def dot(left, right):
    return lax.dot_general(left, right, (((1,), (0,)), ((), ())), preferred_element_type=F32)


def dot_parts(left, right):
    return dot(
        jnp.concatenate([left[i] for i, _ in TERMS], axis=1),
        jnp.concatenate([right[j] for _, j in TERMS], axis=0),
    )


def log_bessel(power):
    inv = lax.rsqrt(jnp.maximum(power, 1e-30))
    rho = power * inv
    small = rho < 3.75
    t = jnp.minimum(power, 3.75 * 3.75) * (1.0 / (3.75 * 3.75))
    small_poly = 1.0 + t * (
        3.5156229
        + t * (3.0899424 + t * (1.2067492 + t * (0.2659732 + t * (0.0360768 + t * 0.0045813))))
    )
    q = jnp.minimum(3.75 * inv, 1.0)
    large_poly = 0.39894228 + q * (
        0.01328592
        + q
        * (
            0.00225319
            + q
            * (
                -0.00157565
                + q
                * (
                    0.00916281
                    + q
                    * (-0.02057706 + q * (0.02635537 + q * (-0.01647633 + q * 0.00392377)))
                )
            )
        )
    )
    inner = jnp.where(small, small_poly, large_poly * lax.rsqrt(jnp.maximum(rho, 3.75)))
    return jnp.where(small, 0.0, rho) + jnp.log(inner)


def turn_vector(period, shift):
    lane = lax.broadcasted_iota(jnp.int32, (1, LANES), 1)
    return lane, period, shift


def phase(index, period):
    wrapped = ((index + period // 2) & (period - 1)) - period // 2
    angle = wrapped.astype(F32) * (2.0 * math.pi / period)
    return jnp.cos(angle), jnp.sin(angle)


def tail_kernel(valid_ref, strain_ref, out_ref):
    rows = out_ref.shape[0]
    first = valid_ref.shape[0] - rows // 8
    for i in range(rows // 8):
        out_ref[8 * i : 8 * i + 8, :] = strain_ref[8 * i : 8 * i + 8, :] * valid_ref[
            first + i
        ].astype(F32)


def early_kernel(len_ref, valid_ref, strain_ref, asd_ref, tmpl_ref, dft_ref, section_ref, bank_ref, gated):
    rows = strain_ref.shape[0]
    for i in range(rows // 8):
        gated[8 * i : 8 * i + 8, :] = strain_ref[8 * i : 8 * i + 8, :] * valid_ref[i].astype(F32)
    frame = jnp.concatenate(
        [gated[pl.ds(0, rows // 2, stride=2), :], gated[pl.ds(1, rows // 2, stride=2), :]], axis=1
    )
    pad = jnp.zeros((FA - rows // 2, FA), BF16)
    frame_parts = [jnp.concatenate([pad, part], axis=0) for part in split(frame)]
    section_ref[0] = dot_parts([dft_ref[0, p] for p in range(PARTS)], frame_parts)
    section_ref[1] = dot_parts([dft_ref[2, p] for p in range(PARTS)], frame_parts)
    lane = lax.broadcasted_iota(jnp.int32, (1, LANES), 1)
    asd = [asd_ref[pl.ds(h, HALF, stride=2), :] for h in range(2)]
    for k in range(tmpl_ref.shape[1]):
        start = OVER - len_ref[k]
        col_cos, col_sin = phase(lane * start, FA)
        energy = jnp.zeros((1, 1), F32)
        turned = []
        for h in range(2):
            re = tmpl_ref[0, k, pl.ds(h, HALF, stride=2), :] * asd[h]
            im = tmpl_ref[1, k, pl.ds(h, HALF, stride=2), :] * asd[h]
            energy += jnp.sum(re * re + im * im, keepdims=True)
            row_cos, row_sin = phase((lane + h * LANES) * start, NFFT)
            new_re = (re * row_cos + im * row_sin).T
            new_im = (re * row_sin - im * row_cos).T
            turned.append((new_re, new_im))
        scale = lax.rsqrt(energy) * (1.0 / math.sqrt(NFFT))
        for h in range(2):
            new_re, new_im = turned[h]
            here = slice(h * HALF, h * HALF + HALF)
            bank_ref[k, here, :HALF] = (new_re * col_cos - new_im * col_sin) * scale
            bank_ref[k, here, HALF:] = (new_re * col_sin + new_im * col_cos) * scale


def spectrum_of(tail_ref, section_ref, head_ref, dft_ref, twist_ref):
    rows = tail_ref.shape[0]
    tail = jnp.concatenate(
        [tail_ref[pl.ds(0, rows // 2, stride=2), :], tail_ref[pl.ds(1, rows // 2, stride=2), :]],
        axis=1,
    )
    tail_parts = split(tail)
    extra = dot(head_ref[...], jnp.concatenate([tail_parts[j] for _, j in TERMS], axis=0))
    re = section_ref[0] + extra[:FA]
    im = section_ref[1] + extra[FA:]
    turn_cos, turn_sin = twist_ref[0], twist_ref[1]
    turned = jnp.concatenate([re * turn_cos + im * turn_sin, im * turn_cos - re * turn_sin], axis=1)
    right = [
        jnp.concatenate(
            [
                jnp.concatenate([dft_ref[0, p, :, :HALF], dft_ref[2, p, :, :HALF]], axis=1),
                jnp.concatenate([dft_ref[1, p, :, :HALF], dft_ref[0, p, :, :HALF]], axis=1),
            ],
            axis=0,
        )
        for p in range(PARTS)
    ]
    return dot_parts(split(turned), right)


def scores_of(spec, bank_k, dft_ref, twist_ref, rows):
    spec_re, spec_im = spec[:, :HALF], spec[:, HALF:]
    bank_re, bank_im = bank_k[:, :HALF], bank_k[:, HALF:]
    prod = jnp.concatenate(
        [spec_re * bank_re - spec_im * bank_im, spec_re * bank_im + spec_im * bank_re], axis=1
    )
    right = [
        jnp.concatenate(
            [
                jnp.concatenate([dft_ref[0, p, :HALF, :], dft_ref[1, p, :HALF, :]], axis=1),
                jnp.concatenate([dft_ref[2, p, :HALF, :], dft_ref[0, p, :HALF, :]], axis=1),
            ],
            axis=0,
        )
        for p in range(PARTS)
    ]
    inner = dot_parts(split(prod), right)
    in_re, in_im = inner[:, :FA], inner[:, FA:]
    turn_cos, turn_sin = twist_ref[0], twist_ref[1]
    twisted = split(
        jnp.concatenate([in_re * turn_cos - in_im * turn_sin, in_re * turn_sin + in_im * turn_cos], axis=0)
    )
    corr_re = dot_parts(
        [jnp.concatenate([dft_ref[0, p, :rows, :], dft_ref[2, p, :rows, :]], axis=1) for p in range(PARTS)],
        twisted,
    )
    corr_im = dot_parts(
        [jnp.concatenate([dft_ref[1, p, :rows, :], dft_ref[0, p, :rows, :]], axis=1) for p in range(PARTS)],
        twisted,
    )
    return log_bessel(corr_re * corr_re + corr_im * corr_im)


def traits_tile(len_ref, weight_ref, chirp_ref, count):
    rows = trait_rows(count)
    row = lax.broadcasted_iota(jnp.int32, (rows, LANES), 0)
    tile = jnp.zeros((rows, LANES), F32)
    for k in range(count):
        tile = jnp.where(row == 3 * k, weight_ref[k], tile)
        tile = jnp.where(row == 3 * k + 1, chirp_ref[k], tile)
        tile = jnp.where(row == 3 * k + 2, len_ref[k].astype(F32) / RATE, tile)
    return tile


def trait_rows(count):
    return (3 * count + 7) // 8 * 8


def partner(me, r, n):
    return me ^ r if n & (n - 1) == 0 else (me + r) % n


def main_kernel(
    len_ref, weight_ref, chirp_ref, tail_ref, section_ref, bank_ref, head_ref, dft_ref, twist_ref, *refs
):
    n = len(refs) - 1
    outs, scores = refs[:n], refs[n]
    count, rows = bank_ref.shape[0], scores.shape[1]
    me = lax.axis_index("bank")
    spec = spectrum_of(tail_ref, section_ref, head_ref, dft_ref, twist_ref)
    for k in range(count):
        score = scores_of(spec, bank_ref[k], dft_ref, twist_ref, rows // 2)
        scores[k, pl.ds(0, rows // 2, stride=2), :] = score[:, :LANES]
        scores[k, pl.ds(1, rows // 2, stride=2), :] = score[:, LANES:]
    share = rows // n
    tile = traits_tile(len_ref, weight_ref, chirp_ref, count)
    for r in range(n):
        begin = pl.multiple_of(partner(me, r, n) * share, 8)
        for k in range(count):
            outs[r][k * share : (k + 1) * share, :] = scores[k, pl.ds(begin, share), :]
        outs[r][count * share :, :] = tile


def final_kernel(*refs):
    *banks, log_ref, chirp_ref, delay_ref = refs
    share = log_ref.shape[0]
    count = banks[0].shape[0] // share
    entries = [
        (
            bank[k * share : (k + 1) * share, :],
            *(bank[count * share + 3 * k + i : count * share + 3 * k + i + 1, :] for i in range(3)),
        )
        for bank in banks
        for k in range(count)
    ]
    peak = functools.reduce(jnp.maximum, [entry[0] for entry in entries])
    masses = [entry[1] * jnp.exp(entry[0] - peak) for entry in entries]
    total = functools.reduce(jnp.add, masses)
    chirp = functools.reduce(jnp.add, [mass * entry[2] for mass, entry in zip(masses, entries)])
    delay = functools.reduce(jnp.add, [mass * entry[3] for mass, entry in zip(masses, entries)])
    prior = functools.reduce(jnp.add, [entry[1] for entry in entries])
    log_ref[...] = peak + jnp.log(total) - jnp.log(prior)
    inv = 1.0 / total
    chirp_ref[...] = chirp * inv
    delay_ref[...] = delay * inv


SMEM = pl.BlockSpec(memory_space=pltpu.SMEM)
VMEM = pl.BlockSpec(memory_space=pltpu.VMEM)
VMEM_LIMIT = 60 * 1024 * 1024


def params():
    return pltpu.CompilerParams(vmem_limit_bytes=VMEM_LIMIT)


def local(strain, inv_asd, templates, tmpl_len, weights, chirp_mass, valid):
    n = lax.axis_size("bank")
    segs = lax.axis_size("seg")
    count = templates.shape[1]
    rows = strain.shape[0] // LANES
    tail_rows = OVER // LANES
    table = tables()
    dft, twist, head = (jnp.asarray(table[key]) for key in ("dft", "twist", "head"))
    strain = strain.reshape(rows, LANES)
    tail = pl.pallas_call(
        tail_kernel,
        grid=(1,),
        in_specs=[SMEM, pl.BlockSpec((tail_rows, LANES), lambda i: (rows // tail_rows - 1, 0))],
        out_specs=VMEM,
        out_shape=pltpu.VMEM((tail_rows, LANES), F32),
        name="tail",
    )(valid, strain)
    halo = lax.ppermute(tail, "seg", [(i, i + 1) for i in range(segs - 1)])
    section, bank = pl.pallas_call(
        early_kernel,
        in_specs=[SMEM, SMEM, VMEM, VMEM, VMEM, VMEM],
        out_specs=[VMEM, VMEM],
        out_shape=[pltpu.VMEM((2, FA, FA), F32), pltpu.VMEM((count, FA, FA), F32)],
        scratch_shapes=[pltpu.VMEM((rows, LANES), F32)],
        compiler_params=params(),
        cost_estimate=pl.CostEstimate(flops=2 * 10**9, bytes_accessed=2 * 10**6, transcendentals=0),
        name="early",
    )(
        tmpl_len,
        valid,
        strain,
        inv_asd.reshape(-1, LANES),
        templates.astype(F32).reshape(2, count, -1, LANES),
        dft,
    )
    share = rows // n
    chunk = (count * share + trait_rows(count), LANES)
    outs = pl.pallas_call(
        main_kernel,
        in_specs=[SMEM] * 3 + [VMEM] * 6,
        out_specs=[VMEM] * n,
        out_shape=[pltpu.VMEM(chunk, F32)] * n,
        scratch_shapes=[pltpu.VMEM((count, rows, LANES), F32)],
        compiler_params=params(),
        cost_estimate=pl.CostEstimate(flops=4 * 10**9, bytes_accessed=4 * 10**6, transcendentals=0),
        name="main",
    )(tmpl_len, weights, chirp_mass, halo, section, bank, head, dft, twist)
    banks = [outs[0]] + [
        lax.ppermute(outs[r], "bank", [(i, partner(i, r, n)) for i in range(n)]) for r in range(1, n)
    ]
    results = pl.pallas_call(
        final_kernel,
        in_specs=[VMEM] * n,
        out_specs=[VMEM] * 3,
        out_shape=[jax.ShapeDtypeStruct((share, LANES), F32)] * 3,
        compiler_params=params(),
        name="final",
    )(*banks)
    return tuple(result.reshape(-1) for result in results)


def solution(mesh):
    placed = (P("seg"), P(), P(None, "bank", None), P("bank"), P("bank"), P("bank"), P("seg"))
    return jax.shard_map(
        local,
        mesh=mesh,
        in_specs=placed,
        out_specs=(P(("seg", "bank")), P(("seg", "bank")), P(("seg", "bank"))),
        check_vma=False,
    )
```

time: 71.6 us -> 29.5 us (0.41)
  matrix products: 22.9 us -> 0 us
  local copies, waits for them, and re-layouts: 20.1 us -> 5.39 us
  Pallas kernels: 0 us -> 11.2 us
  other arithmetic: 8.63 us -> 0 us
  starting transfers between devices: 11.6 us -> 6.73 us
  between operations: 1.69 us -> 0.68 us
    dot_general x14 -> x0, matrix products: 22.9 us -> none  [the longest x4 7.51 us: contract_last(): lax.dot_general(left_mat, right_mat, (((1,), (1,)), ((), ())), precision=...]
    gather x8 -> x0, local copies, waits for them, and re-layouts: 13.4 us -> none
    pallas_call x0 -> x4, Pallas kernels: none -> 11.2 us  [the longest x1 6.28 us: local(): pl.pallas_call(main_kernel, in_specs=[SMEM] * 3 + [VMEM] * 6, out_specs=[...]
    all_to_all x2 -> x0, starting transfers between devices: 6.71 us -> none  [the longest x1 3.46 us: local(): lax.all_to_all(aligned, 'bank', split_axis=1, concat_axis=0, tiled=True)]
    all_to_all x2 -> x0, waiting for transfers between devices: 5.77 us -> none  [the longest x1 5.76 us: local(): lax.all_to_all(aligned, 'bank', split_axis=1, concat_axis=0, tiled=True)]
    ppermute x1 -> x4, waiting for transfers between devices: 0.01 us -> 5.16 us  [the longest x3 5.16 us: local(): lax.ppermute(outs[r], 'bank', [(i, partner(i, r, n)) for i in range(n)])]
    select_n x1 -> x0, other arithmetic: 3.79 us -> none  [log_bessel(): return jnp.where(rho_val < 3.75, jnp.log(small_poly), large_val)]
    ppermute x1 -> x4, starting transfers between devices: 4.87 us -> 6.73 us  [the longest x1 4.87 us: local(): halo = lax.ppermute(tail, 'seg', [(i, i + 1) for i in range(segs - 1)])]
  transfers between devices with their start and end apart: 3 -> 4, of which waited for: 1 -> 2; matrix products, arithmetic and copies ran while one was open for 63% -> 7% of each run, Pallas kernels for 0% -> 8%
where the time goes in v1:
time: 29.5 us; the launch traced here: 29.2 us
  Pallas kernels  11.2 us (38%)
  starting transfers between devices  6.73 us (23%)
  local copies, waits for them, and re-layouts  5.39 us (18%)
  waiting for transfers between devices  5.16 us (17%)
  between operations  0.68 us (2%)
    pallas_call x1, Pallas kernels, local(): pl.pallas_call(main_kernel, in_specs=[SMEM] * 3 + [VMEM] * 6, out_specs=[...  6.28 us
    ppermute x3, waiting for transfers between devices, local(): lax.ppermute(outs[r], 'bank', [(i, partner(i, r, n)) for i in range(n)])  5.16 us
    ppermute x1, starting transfers between devices, local(): halo = lax.ppermute(tail, 'seg', [(i, i + 1) for i in range(segs - 1)])  4.87 us
    unnamed x14, local copies, waits for them, and re-layouts  3.47 us
    pallas_call x1, Pallas kernels, local(): pl.pallas_call(early_kernel, in_specs=[SMEM, SMEM, VMEM, VMEM, VMEM, VMEM...  2.24 us
    reshape x1, local copies, waits for them, and re-layouts, local(): templates.astype(F32).reshape(2, count, -1, LANES)  1.92 us
    ppermute x3, starting transfers between devices, local(): lax.ppermute(outs[r], 'bank', [(i, partner(i, r, n)) for i in range(n)])  1.86 us
    pallas_call x1, Pallas kernels, local(): pl.pallas_call(final_kernel, in_specs=[VMEM] * n, out_specs=[VMEM] * 3, o...  1.82 us
  transfers between devices with their start and end apart: 4, of which 2 were waited for; matrix products, arithmetic and copies ran while one was open for 7% of the time, Pallas kernels for 8%

profile of v1, /device:TPU:0, one launch (start us, length us, event | category | flops | bytes accessed | tf_op | source)
XLA Modules:
  0.0 29.2 jit_solution(12866111214322389378)
XLA Ops:
  0.6 0.9 %tail.1 = f32[128,128]{1,0:T(8,128)S(1)} custom-call(s32[48]{0:T(128)} %valid_ref.3, f32[384,128]{1,0:T(8,128)} %bitcast.5), custom_call_target="tpu_custom_call" | custom-call | tf_op jit(solution)/shard_map/tail/pallas_call | solution.py:302
  1.5 4.9 %collective-permute-start = (f32[128,128]{1,0:T(8,128)S(1)}, f32[128,128]{1,0:T(8,128)S(1)}, u32[]{:S(2)}, u32[]{:S(2)}) collective-permute-start(f32[128,128]{1,0:T(8,128)S(1)} %tail.1), channel_id=1, source_target_pairs={{0,4},{4,8},{8,12},{12,16},{16,20},{20,24},{24,28},{1,5},{5,9},{9,... | collective-permute-start | bytes 196616 | tf_op jit(solution)/shard_map/ppermute | solution.py:310
  6.4 1.9 %reshape.34.tmpl_ref = f32[2,2,256,128]{3,2,1,0:T(8,128)} reshape(bf16[2,2,32768]{2,1,0:T(2,128)(2,1)} %param.12) | data formatting | bytes 786432 | tf_op jit(solution)/shard_map/reshape | solution.py:325
  8.3 2.2 %early.1 = (f32[2,256,256]{2,1,0:T(8,128)S(1)}, f32[2,256,256]{2,1,0:T(8,128)S(1)}) custom-call(s32[2]{0:T(128)} %len_ref.3, s32[48]{0:T(128)} %valid_ref.3, f32[384,128]{1,0:T(8,128)} %bitcast.6, f32[256,128]{1,0:T(8,128)} %bitcast.7, f32[2,2,256,128]{3,2,1,0:T(8,128)} %reshape.34.tmpl_ref, bf16[3,3,256,256]{3,2,1,0:T(8,128)(2,1)} %constant.6.clone.dft_ref), custom_call_target="tpu_custom_call" | custom-call | flops 2000000000 | bytes 2000000 | tf_op jit(solution)/shard_map/early/pallas_call | solution.py:311
  10.5 0.0 copy-start.1
  10.6 0.8 %copy-done.1 = f32[2,256,256]{2,1,0:T(8,128)} copy-done((f32[2,256,256]{2,1,0:T(8,128)}, f32[2,256,256]{2,1,0:T(8,128)S(1)}, u32[]{:S(2)}) %copy-start.1) | copy-done | bytes 524312
  11.3 0.0 copy-start.2
  11.3 0.8 %copy-done.2 = f32[2,256,256]{2,1,0:T(8,128)} copy-done((f32[2,256,256]{2,1,0:T(8,128)}, f32[2,256,256]{2,1,0:T(8,128)S(1)}, u32[]{:S(2)}) %copy-start.2) | copy-done | bytes 524312
  12.1 0.0 collective-permute-done.tail_ref
  12.1 0.0 copy-start.6
  12.1 0.6 %copy-done.6 = f32[128,128]{1,0:T(8,128)} copy-done((f32[128,128]{1,0:T(8,128)}, f32[128,128]{1,0:T(8,128)S(1)}, u32[]{:S(2)}) %copy-start.6) | copy-done | bytes 65560
  12.8 6.3 %main.1 = (f32[200,128]{1,0:T(8,128)S(1)}, f32[200,128]{1,0:T(8,128)S(1)}, f32[200,128]{1,0:T(8,128)S(1)}, f32[200,128]{1,0:T(8,128)S(1)}) custom-call(s32[2]{0:T(128)} %len_ref.3, f32[2]{0:T(128)} %weight_ref.1, f32[2]{0:T(128)} %chirp_ref.1, f32[128,128]{1,0:T(8,128)} %copy-done.6, f32[2,256,256]{2,1,0:T(8,128)} %copy-done.1, f32[2,256,256]{2,1,0:T(8,128)} %copy-done.2, ...), custom_call_target="tpu_custom_call" | custom-call | flops 4000000000 | bytes 4000000 | tf_op jit(solution)/shard_map/main/pallas_call | solution.py:330
  19.1 0.0 copy-start
  19.1 0.6 %copy-done = f32[200,128]{1,0:T(8,128)} copy-done((f32[200,128]{1,0:T(8,128)}, f32[200,128]{1,0:T(8,128)S(1)}, u32[]{:S(2)}) %copy-start) | copy-done | bytes 102424
  19.7 0.0 collective-permute-start.1
  19.7 1.5 %collective-permute-start.2 = (f32[200,128]{1,0:T(8,128)S(1)}, f32[200,128]{1,0:T(8,128)S(1)}, u32[]{:S(2)}, u32[]{:S(2)}) collective-permute-start(f32[200,128]{1,0:T(8,128)S(1)} %get-tuple-element.16), channel_id=1, source_target_pairs={{0,2},{1,3},{2,0},{3,1},{4,6},{5,7},{6,4},{7,5},{8,10},{9,11},{10,... | collective-permute-start | bytes 307208 | tf_op jit(solution)/shard_map/ppermute | solution.py:341
  21.2 0.3 %collective-permute-start.3 = (f32[200,128]{1,0:T(8,128)S(1)}, f32[200,128]{1,0:T(8,128)S(1)}, u32[]{:S(2)}, u32[]{:S(2)}) collective-permute-start(f32[200,128]{1,0:T(8,128)S(1)} %get-tuple-element.17), channel_id=1, source_target_pairs={{0,3},{1,2},{2,1},{3,0},{4,7},{5,6},{6,5},{7,4},{8,11},{9,10},{10,... | collective-permute-start | bytes 307208 | tf_op jit(solution)/shard_map/ppermute | solution.py:341
  21.5 0.0 collective-permute-done.1.refs_1_
  21.6 0.0 copy-start.3
  21.6 3.9 %collective-permute-done.2.refs_2_ = f32[200,128]{1,0:T(8,128)S(1)} collective-permute-done((f32[200,128]{1,0:T(8,128)S(1)}, f32[200,128]{1,0:T(8,128)S(1)}, u32[]{:S(2)}, u32[]{:S(2)}) %collective-permute-start.2) | collective-permute-done | bytes 102432 | tf_op jit(solution)/shard_map/ppermute | solution.py:341
  25.4 0.0 copy-start.4
  25.4 1.3 %collective-permute-done.3.refs_3_ = f32[200,128]{1,0:T(8,128)S(1)} collective-permute-done((f32[200,128]{1,0:T(8,128)S(1)}, f32[200,128]{1,0:T(8,128)S(1)}, u32[]{:S(2)}, u32[]{:S(2)}) %collective-permute-start.3) | collective-permute-done | bytes 102432 | tf_op jit(solution)/shard_map/ppermute | solution.py:341
  26.7 0.0 copy-start.5
  26.7 0.0 copy-done.3
  26.7 0.0 copy-done.4
  26.7 0.6 %copy-done.5 = f32[200,128]{1,0:T(8,128)} copy-done((f32[200,128]{1,0:T(8,128)}, f32[200,128]{1,0:T(8,128)S(1)}, u32[]{:S(2)}) %copy-start.5) | copy-done | bytes 102424
  27.4 1.8 %final.1 = (f32[96,128]{1,0:T(8,128)}, f32[96,128]{1,0:T(8,128)}, f32[96,128]{1,0:T(8,128)}) custom-call(f32[200,128]{1,0:T(8,128)} %copy-done, f32[200,128]{1,0:T(8,128)} %copy-done.3, f32[200,128]{1,0:T(8,128)} %copy-done.4, f32[200,128]{1,0:T(8,128)} %copy-done.5), custom_call_target="tpu_custom_call" | custom-call | tf_op jit(solution)/shard_map/final/pallas_call | solution.py:343
Async XLA Ops:
  1.5 10.6 %collective-permute-start = (f32[128,128]{1,0:T(8,128)S(1)}, f32[128,128]{1,0:T(8,128)S(1)}, u32[]{:S(2)}, u32[]{:S(2)}) collective-permute-start(f32[128,128]{1,0:T(8,128)S(1)} %tail.1), channel_id=1, source_target_pairs={{0,4},{4,8},{8,12},{12,16},{16,20},{20,24},{24,28},{1,5},{5,9},{9,... | collective-permute-start | bytes 196616 | tf_op jit(solution)/shard_map/ppermute | solution.py:310
  10.5 0.8 %copy-start.1 = (f32[2,256,256]{2,1,0:T(8,128)}, f32[2,256,256]{2,1,0:T(8,128)S(1)}, u32[]{:S(2)}) copy-start(f32[2,256,256]{2,1,0:T(8,128)S(1)} %get-tuple-element.12.section_ref) | copy-start | bytes 1572868
  11.3 0.8 %copy-start.2 = (f32[2,256,256]{2,1,0:T(8,128)}, f32[2,256,256]{2,1,0:T(8,128)S(1)}, u32[]{:S(2)}) copy-start(f32[2,256,256]{2,1,0:T(8,128)S(1)} %get-tuple-element.13.bank_ref) | copy-start | bytes 1572868
  12.1 0.6 %copy-start.6 = (f32[128,128]{1,0:T(8,128)}, f32[128,128]{1,0:T(8,128)S(1)}, u32[]{:S(2)}) copy-start(f32[128,128]{1,0:T(8,128)S(1)} %collective-permute-done.tail_ref) | copy-start | bytes 196612
  19.1 0.6 %copy-start = (f32[200,128]{1,0:T(8,128)}, f32[200,128]{1,0:T(8,128)S(1)}, u32[]{:S(2)}) copy-start(f32[200,128]{1,0:T(8,128)S(1)} %get-tuple-element.14.refs_0_) | copy-start | bytes 307204
  19.7 1.9 %collective-permute-start.1 = (f32[200,128]{1,0:T(8,128)S(1)}, f32[200,128]{1,0:T(8,128)S(1)}, u32[]{:S(2)}, u32[]{:S(2)}) collective-permute-start(f32[200,128]{1,0:T(8,128)S(1)} %get-tuple-element.15), channel_id=1, source_target_pairs={{0,1},{1,0},{2,3},{3,2},{4,5},{5,4},{6,7},{7,6},{8,9},{9,8},{10,11... | collective-permute-start | bytes 307208 | tf_op jit(solution)/shard_map/ppermute | solution.py:341
  19.7 5.8 %collective-permute-start.2 = (f32[200,128]{1,0:T(8,128)S(1)}, f32[200,128]{1,0:T(8,128)S(1)}, u32[]{:S(2)}, u32[]{:S(2)}) collective-permute-start(f32[200,128]{1,0:T(8,128)S(1)} %get-tuple-element.16), channel_id=1, source_target_pairs={{0,2},{1,3},{2,0},{3,1},{4,6},{5,7},{6,4},{7,5},{8,10},{9,11},{10,... | collective-permute-start | bytes 307208 | tf_op jit(solution)/shard_map/ppermute | solution.py:341
  21.2 5.5 %collective-permute-start.3 = (f32[200,128]{1,0:T(8,128)S(1)}, f32[200,128]{1,0:T(8,128)S(1)}, u32[]{:S(2)}, u32[]{:S(2)}) collective-permute-start(f32[200,128]{1,0:T(8,128)S(1)} %get-tuple-element.17), channel_id=1, source_target_pairs={{0,3},{1,2},{2,1},{3,0},{4,7},{5,6},{6,5},{7,4},{8,11},{9,10},{10,... | collective-permute-start | bytes 307208 | tf_op jit(solution)/shard_map/ppermute | solution.py:341
  21.6 5.2 %copy-start.3 = (f32[200,128]{1,0:T(8,128)}, f32[200,128]{1,0:T(8,128)S(1)}, u32[]{:S(2)}) copy-start(f32[200,128]{1,0:T(8,128)S(1)} %collective-permute-done.1.refs_1_) | copy-start | bytes 307204
  25.4 1.3 %copy-start.4 = (f32[200,128]{1,0:T(8,128)}, f32[200,128]{1,0:T(8,128)S(1)}, u32[]{:S(2)}) copy-start(f32[200,128]{1,0:T(8,128)S(1)} %collective-permute-done.2.refs_2_) | copy-start | bytes 307204
  26.7 0.6 %copy-start.5 = (f32[200,128]{1,0:T(8,128)}, f32[200,128]{1,0:T(8,128)S(1)}, u32[]{:S(2)}) copy-start(f32[200,128]{1,0:T(8,128)S(1)} %collective-permute-done.3.refs_3_) | copy-start | bytes 307204

commit v2 on v1

v2 whole, which is shorter than its diff:
```python
import functools
import math

import jax
import jax.numpy as jnp
import numpy as np
from jax import lax
from jax.experimental import pallas as pl
from jax.experimental.pallas import tpu as pltpu
from jax.sharding import PartitionSpec as P

NFFT = 65536
FA = 256
HALF = 128
OVER = 16384
RATE = 4096
LANES = 128
F32 = jnp.float32
BF16 = jnp.bfloat16

TERMS = ((0, 0), (0, 1), (1, 0), (1, 1), (0, 2), (2, 0))
PARTS = 1 + max(max(term) for term in TERMS)


def parts_of_table(table):
    rest = np.asarray(table, np.float32)
    parts = []
    for _ in range(PARTS):
        part = rest.astype(jnp.bfloat16)
        parts.append(part)
        rest = rest - part.astype(np.float32)
    return parts


def complex_rows(angle, sign):
    cos, sin = np.cos(angle), sign * np.sin(angle)
    return np.block([[cos, -sin], [sin, cos]])


@functools.cache
def tables(hop_rows):
    index = np.arange(FA)
    grid = index[:, None] * index[None, :]
    full = 2.0 * math.pi / FA
    first = parts_of_table(np.concatenate([np.cos(grid % FA * full), -np.sin(grid % FA * full)]))
    rows = OVER // FA
    head = np.concatenate([first[i][:, :rows] for i, _ in TERMS], axis=1)
    quarter = np.arange(FA // 4)
    second = np.concatenate(
        [
            complex_rows((2 * quarter[:, None] + odd) * index[None, :] % FA * full, -1.0).T
            for odd in range(2)
        ],
        axis=1,
    )
    second = np.concatenate([part for part in parts_of_table(second)])
    third = []
    for odd in range(2):
        angle = index[:HALF, None] * (2 * quarter[None, :] + odd) % FA * full
        parts = parts_of_table(complex_rows(angle, 1.0).T)
        third.append(np.stack(parts))
    angle = np.arange(hop_rows // 2)[:, None] * index[None, :HALF] % HALF * (2.0 * full)
    fourth = parts_of_table(complex_rows(angle, 1.0))
    fine = grid * (2.0 * math.pi / NFFT)
    turn = np.repeat(index[:HALF, None] * full, LANES, axis=1)
    return {
        "first": np.stack(first),
        "head": head,
        "second": second.reshape(PARTS, 2 * FA, FA),
        "third": np.stack(third),
        "fourth": np.stack(fourth),
        "twist": np.stack([np.cos(fine), np.sin(fine)]).astype(np.float32),
        "turn": np.stack([np.cos(turn), np.sin(turn)]).astype(np.float32),
    }


def split(value):
    parts = []
    for step in range(PARTS):
        part = value.astype(BF16)
        parts.append(part)
        if step < PARTS - 1:
            value = value - part.astype(F32)
    return parts


def dot(left, right):
    return lax.dot_general(left, right, (((1,), (0,)), ((), ())), preferred_element_type=F32)


def left_terms(parts):
    return jnp.concatenate([parts[i] for i, _ in TERMS], axis=1)


def right_terms(parts):
    return jnp.concatenate([parts[j] for _, j in TERMS], axis=0)


def log_bessel(power):
    inv = lax.rsqrt(jnp.maximum(power, 1e-30))
    rho = power * inv
    small = rho < 3.75
    t = jnp.minimum(power, 3.75 * 3.75) * (1.0 / (3.75 * 3.75))
    small_poly = 1.0 + t * (
        3.5156229
        + t * (3.0899424 + t * (1.2067492 + t * (0.2659732 + t * (0.0360768 + t * 0.0045813))))
    )
    q = jnp.minimum(3.75 * inv, 1.0)
    large_poly = 0.39894228 + q * (
        0.01328592
        + q
        * (
            0.00225319
            + q
            * (
                -0.00157565
                + q
                * (
                    0.00916281
                    + q
                    * (-0.02057706 + q * (0.02635537 + q * (-0.01647633 + q * 0.00392377)))
                )
            )
        )
    )
    inner = jnp.where(small, small_poly, large_poly * lax.rsqrt(jnp.maximum(rho, 3.75)))
    return jnp.where(small, 0.0, rho) + jnp.log(inner)


def phase(index, period):
    wrapped = ((index + period // 2) & (period - 1)) - period // 2
    angle = wrapped.astype(F32) * (2.0 * math.pi / period)
    return jnp.cos(angle), jnp.sin(angle)


def gate(target, source, flags, first):
    for i in range(target.shape[0] // 8):
        here = slice(8 * i, 8 * i + 8)
        target[here, :] = source[here, :] * flags[first + i].astype(F32)


def frame_of(samples):
    rows = samples.shape[0] // 2
    return jnp.concatenate([samples[pl.ds(h, rows, stride=2), :] for h in range(2)], axis=1)


def tail_kernel(valid_hbm, strain_hbm, out_ref, samples, flags, sems):
    rows = samples.shape[0]
    copies = [
        pltpu.make_async_copy(strain_hbm.at[pl.ds(strain_hbm.shape[0] - rows, rows), :], samples, sems.at[0]),
        pltpu.make_async_copy(valid_hbm, flags, sems.at[1]),
    ]
    for copy in copies:
        copy.start()
    for copy in copies:
        copy.wait()
    gate(out_ref, samples, flags, flags.shape[0] - rows // 8)


def early_kernel(
    len_hbm,
    weight_hbm,
    chirp_hbm,
    valid_hbm,
    strain_hbm,
    asd_hbm,
    first_hbm,
    tmpl_ref,
    section_ref,
    bank_ref,
    traits_ref,
    lens,
    weights,
    chirps,
    flags,
    samples,
    gated,
    asd_v,
    first_v,
    sems,
):
    pairs = (
        (strain_hbm, samples),
        (valid_hbm, flags),
        (first_hbm, first_v),
        (asd_hbm, asd_v),
        (len_hbm, lens),
        (weight_hbm, weights),
        (chirp_hbm, chirps),
    )
    copies = [pltpu.make_async_copy(a, b, sems.at[i]) for i, (a, b) in enumerate(pairs)]
    for copy in copies:
        copy.start()
    for copy in copies:
        copy.wait()
    gate(gated, samples, flags, 0)
    frame = frame_of(gated)
    pad = jnp.zeros((FA - frame.shape[0], FA), BF16)
    frame_parts = [jnp.concatenate([pad, part], axis=0) for part in split(frame)]
    section_ref[...] = dot(left_terms([first_v[p] for p in range(PARTS)]), right_terms(frame_parts))
    traits_ref[...] = traits_tile(lens, weights, chirps, tmpl_ref.shape[1])
    lane = lax.broadcasted_iota(jnp.int32, (1, LANES), 1)
    quarter = FA // 4
    sign = jnp.where(lane < quarter, 1.0, -1.0)
    blocks = [(q, h) for q in range(2) for h in range(2)]
    asd = {(q, h): asd_v[pl.ds(2 * q + h, quarter, stride=4), :] for q, h in blocks}
    for k in range(tmpl_ref.shape[1]):
        start = OVER - lens[k]
        energy = jnp.zeros((1, 1), F32)
        turned = {}
        for q, h in blocks:
            re = tmpl_ref[0, k, pl.ds(2 * q + h, quarter, stride=4), :] * asd[q, h]
            im = tmpl_ref[1, k, pl.ds(2 * q + h, quarter, stride=4), :] * asd[q, h]
            energy += jnp.sum(re * re + im * im, keepdims=True)
            row_cos, row_sin = phase((lane + h * LANES) * start, NFFT)
            new_re = re * row_cos + im * row_sin
            new_im = re * row_sin - im * row_cos
            turned[q, h] = (
                jnp.concatenate([new_re, new_re], axis=0).T,
                jnp.concatenate([-new_im, new_im], axis=0).T,
            )
        scale = lax.rsqrt(energy) * (1.0 / math.sqrt(NFFT))
        for q in range(2):
            col_cos, col_sin = phase((2 * (lane & (quarter - 1)) + q) * start, FA)
            col_cos, col_sin = col_cos * scale, col_sin * sign * scale
            for h in range(2):
                own, cross = turned[q, h]
                rows, cols = slice(h * HALF, h * HALF + HALF), slice(q * LANES, q * LANES + LANES)
                bank_ref[k, 0, rows, cols] = own * col_cos + cross * col_sin
                bank_ref[k, 1, rows, cols] = cross * col_cos - own * col_sin


def spectrum_of(tail_ref, section_ref, head_ref, second_ref, twist_ref):
    section = section_ref[...] + dot(head_ref[...], right_terms(split(frame_of(tail_ref))))
    re, im = section[:FA], section[FA:]
    turn_cos, turn_sin = twist_ref[0], twist_ref[1]
    turned = jnp.concatenate([re * turn_cos + im * turn_sin, im * turn_cos - re * turn_sin], axis=1)
    return dot(left_terms(split(turned)), right_terms([second_ref[p] for p in range(PARTS)]))


def swapped(value):
    return jnp.concatenate(
        [pltpu.roll(value[:, i : i + LANES], LANES // 2, axis=1) for i in range(0, value.shape[1], LANES)],
        axis=1,
    )


def scores_of(spec, spec_swapped, bank_ref, k, third_ref, fourth_ref, twist_ref, turn_ref):
    prod = spec * bank_ref[k, 0] + spec_swapped * bank_ref[k, 1]
    even = dot(left_terms(split(prod[:, :LANES])), right_terms([third_ref[0, p] for p in range(PARTS)]))
    odd = dot(left_terms(split(prod[:, LANES:])), right_terms([third_ref[1, p] for p in range(PARTS)]))
    plus, minus = even + odd, even - odd
    in_re = jnp.concatenate([plus[:, :HALF], minus[:, :HALF]], axis=1)
    in_im = jnp.concatenate([plus[:, HALF:], minus[:, HALF:]], axis=1)
    turn_cos, turn_sin = twist_ref[0], twist_ref[1]
    out_re = in_re * turn_cos - in_im * turn_sin
    out_im = in_re * turn_sin + in_im * turn_cos
    sum_re, sum_im = out_re[:HALF] + out_re[HALF:], out_im[:HALF] + out_im[HALF:]
    gap_re, gap_im = out_re[:HALF] - out_re[HALF:], out_im[:HALF] - out_im[HALF:]
    half_cos = jnp.concatenate([turn_ref[0]] * 2, axis=1)
    half_sin = jnp.concatenate([turn_ref[1]] * 2, axis=1)
    odd_re, odd_im = gap_re * half_cos - gap_im * half_sin, gap_re * half_sin + gap_im * half_cos
    pieces = [jnp.concatenate([sum_re, sum_im], axis=0), jnp.concatenate([odd_re, odd_im], axis=0)]
    scores = []
    for piece in pieces:
        corr = dot(left_terms([fourth_ref[p] for p in range(PARTS)]), right_terms(split(piece)))
        rows = corr.shape[0] // 2
        re, im = corr[:rows], corr[rows:]
        scores.append(log_bessel(re * re + im * im))
    return scores


def traits_tile(lens, weights, chirps, count):
    rows = trait_rows(count)
    row = lax.broadcasted_iota(jnp.int32, (rows, LANES), 0)
    tile = jnp.zeros((rows, LANES), F32)
    for k in range(count):
        tile = jnp.where(row == 3 * k, weights[k], tile)
        tile = jnp.where(row == 3 * k + 1, chirps[k], tile)
        tile = jnp.where(row == 3 * k + 2, lens[k].astype(F32) / RATE, tile)
    return tile


def trait_rows(count):
    return (3 * count + 7) // 8 * 8


def partner(me, r, n):
    return me ^ r if n & (n - 1) == 0 else (me + r) % n


def main_kernel(
    tail_ref,
    section_ref,
    bank_ref,
    traits_ref,
    head_ref,
    second_ref,
    third_ref,
    fourth_ref,
    twist_ref,
    turn_ref,
    *refs,
):
    n = len(refs) - 1
    outs, scores = refs[:n], refs[n]
    count, rows = bank_ref.shape[0], scores.shape[1]
    me = lax.axis_index("bank")
    spec = spectrum_of(tail_ref, section_ref, head_ref, second_ref, twist_ref)
    spec_swapped = swapped(spec)
    for k in range(count):
        pair = scores_of(spec, spec_swapped, bank_ref, k, third_ref, fourth_ref, twist_ref, turn_ref)
        for q, score in enumerate(pair):
            for h in range(2):
                scores[k, pl.ds(2 * q + h, rows // 4, stride=4), :] = score[:, h * LANES : (h + 1) * LANES]
    share = rows // n
    for r in range(n):
        begin = pl.multiple_of(partner(me, r, n) * share, 8)
        for k in range(count):
            outs[r][k * share : (k + 1) * share, :] = scores[k, pl.ds(begin, share), :]
        outs[r][count * share :, :] = traits_ref[...]


def final_kernel(*refs):
    *banks, log_ref, chirp_ref, delay_ref = refs
    share = log_ref.shape[0]
    count = banks[0].shape[0] // share
    entries = [
        (
            bank[k * share : (k + 1) * share, :],
            *(bank[count * share + 3 * k + i : count * share + 3 * k + i + 1, :] for i in range(3)),
        )
        for bank in banks
        for k in range(count)
    ]
    peak = functools.reduce(jnp.maximum, [entry[0] for entry in entries])
    masses = [entry[1] * jnp.exp(entry[0] - peak) for entry in entries]
    total = functools.reduce(jnp.add, masses)
    chirp = functools.reduce(jnp.add, [mass * entry[2] for mass, entry in zip(masses, entries)])
    delay = functools.reduce(jnp.add, [mass * entry[3] for mass, entry in zip(masses, entries)])
    prior = functools.reduce(jnp.add, [entry[1] for entry in entries])
    log_ref[...] = peak + jnp.log(total) - jnp.log(prior)
    inv = 1.0 / total
    chirp_ref[...] = chirp * inv
    delay_ref[...] = delay * inv


HBM = pl.BlockSpec(memory_space=pltpu.HBM)
VMEM = pl.BlockSpec(memory_space=pltpu.VMEM)


def in_hbm(value):
    return pltpu.with_memory_space_constraint(value, pltpu.HBM)


def params(mib):
    return pltpu.CompilerParams(vmem_limit_bytes=mib * 1024 * 1024)


def local(strain, inv_asd, templates, tmpl_len, weights, chirp_mass, valid):
    n = lax.axis_size("bank")
    segs = lax.axis_size("seg")
    count = templates.shape[1]
    rows = strain.shape[0] // LANES
    tail_rows = OVER // LANES
    flags = valid.shape[0]
    table = {key: jnp.asarray(value) for key, value in tables(rows // 2).items()}
    tmpl_len, weights, chirp_mass, valid = map(in_hbm, (tmpl_len, weights, chirp_mass, valid))
    strain = in_hbm(strain.reshape(rows, LANES))
    asd = in_hbm(inv_asd.reshape(-1, LANES))
    tail = pl.pallas_call(
        tail_kernel,
        in_specs=[HBM] * 2,
        out_specs=VMEM,
        out_shape=pltpu.VMEM((tail_rows, LANES), F32),
        scratch_shapes=[
            pltpu.VMEM((tail_rows, LANES), F32),
            pltpu.SMEM((flags,), jnp.int32),
            pltpu.SemaphoreType.DMA((2,)),
        ],
        compiler_params=params(4),
        name="tail",
    )(valid, strain)
    halo = lax.ppermute(tail, "seg", [(i, i + 1) for i in range(segs - 1)])
    section, bank, traits = pl.pallas_call(
        early_kernel,
        in_specs=[HBM] * 7 + [VMEM],
        out_specs=[VMEM] * 3,
        out_shape=[
            pltpu.VMEM((2 * FA, FA), F32),
            pltpu.VMEM((count, 2, FA, FA), F32),
            pltpu.VMEM((trait_rows(count), LANES), F32),
        ],
        scratch_shapes=[
            pltpu.SMEM((count,), jnp.int32),
            pltpu.SMEM((count,), F32),
            pltpu.SMEM((count,), F32),
            pltpu.SMEM((flags,), jnp.int32),
            pltpu.VMEM((rows, LANES), F32),
            pltpu.VMEM((rows, LANES), F32),
            pltpu.VMEM(asd.shape, F32),
            pltpu.VMEM(table["first"].shape, BF16),
            pltpu.SemaphoreType.DMA((7,)),
        ],
        compiler_params=params(16),
        cost_estimate=pl.CostEstimate(flops=2 * 10**9, bytes_accessed=2 * 10**6, transcendentals=0),
        name="early",
    )(
        tmpl_len,
        weights,
        chirp_mass,
        valid,
        strain,
        asd,
        in_hbm(table["first"]),
        templates.astype(F32).reshape(2, count, -1, LANES),
    )
    share = rows // n
    chunk = (count * share + trait_rows(count), LANES)
    outs = pl.pallas_call(
        main_kernel,
        in_specs=[VMEM] * 10,
        out_specs=[VMEM] * n,
        out_shape=[pltpu.VMEM(chunk, F32)] * n,
        scratch_shapes=[pltpu.VMEM((count, rows, LANES), F32)],
        compiler_params=params(20),
        cost_estimate=pl.CostEstimate(flops=4 * 10**9, bytes_accessed=4 * 10**6, transcendentals=0),
        name="main",
    )(
        halo,
        section,
        bank,
        traits,
        *(table[key] for key in ("head", "second", "third", "fourth", "twist", "turn")),
    )
    banks = [outs[0]] + [
        lax.ppermute(outs[r], "bank", [(i, partner(i, r, n)) for i in range(n)]) for r in range(1, n)
    ]
    results = pl.pallas_call(
        final_kernel,
        in_specs=[VMEM] * n,
        out_specs=[VMEM] * 3,
        out_shape=[jax.ShapeDtypeStruct((share, LANES), F32)] * 3,
        compiler_params=params(8),
        name="final",
    )(*banks)
    return tuple(result.reshape(-1) for result in results)


def solution(mesh):
    placed = (P("seg"), P(), P(None, "bank", None), P("bank"), P("bank"), P("bank"), P("seg"))
    return jax.shard_map(
        local,
        mesh=mesh,
        in_specs=placed,
        out_specs=(P(("seg", "bank")), P(("seg", "bank")), P(("seg", "bank"))),
        check_vma=False,
    )
```

time: 29.5 us -> 20.8 us (0.71)
  local copies, waits for them, and re-layouts: 5.39 us -> 0.22 us
  Pallas kernels: 11.2 us -> 7.52 us
    unnamed x14, local copies, waits for them, and re-layouts: 3.47 us -> 0.05 us
    pallas_call x3, Pallas kernels: 9.38 us -> 6.74 us  [the longest x1 3.61 us: local(): pl.pallas_call(main_kernel, in_specs=[VMEM] * 10, out_specs=[VMEM] * n, o...]
    reshape x1, local copies, waits for them, and re-layouts: 1.92 us -> 0.17 us  [local(): templates.astype(F32).reshape(2, count, -1, LANES)]
    pallas_call x1, Pallas kernels: 1.82 us -> 0.78 us  [local(): pl.pallas_call(final_kernel, in_specs=[VMEM] * n, out_specs=[VMEM] * 3, o...]
  transfers between devices with their start and end apart: 4 -> 4, of which waited for: 2 -> 2; matrix products, arithmetic and copies ran while one was open for 7% -> 1% of each run, Pallas kernels for 8% -> 11%
where the time goes in v2:
time: 20.8 us; the launch traced here: 20.4 us
  Pallas kernels  7.52 us (36%)
  starting transfers between devices  6.79 us (33%)
  waiting for transfers between devices  5.09 us (24%)
  between operations  0.8 us (4%)
  local copies, waits for them, and re-layouts  0.22 us (1%)
    ppermute x3, waiting for transfers between devices, local(): lax.ppermute(outs[r], 'bank', [(i, partner(i, r, n)) for i in range(n)])  5.09 us
    ppermute x1, starting transfers between devices, local(): halo = lax.ppermute(tail, 'seg', [(i, i + 1) for i in range(segs - 1)])  4.87 us
    pallas_call x1, Pallas kernels, local(): pl.pallas_call(main_kernel, in_specs=[VMEM] * 10, out_specs=[VMEM] * n, o...  3.61 us
    pallas_call x1, Pallas kernels, local(): pl.pallas_call(early_kernel, in_specs=[HBM] * 7 + [VMEM], out_specs=[VMEM...  2.21 us
    ppermute x3, starting transfers between devices, local(): lax.ppermute(outs[r], 'bank', [(i, partner(i, r, n)) for i in range(n)])  1.92 us
    pallas_call x1, Pallas kernels, local(): pl.pallas_call(tail_kernel, in_specs=[HBM] * 2, out_specs=VMEM, out_shape...  0.92 us
    pallas_call x1, Pallas kernels, local(): pl.pallas_call(final_kernel, in_specs=[VMEM] * n, out_specs=[VMEM] * 3, o...  0.78 us
  transfers between devices with their start and end apart: 4, of which 2 were waited for; matrix products, arithmetic and copies ran while one was open for 1% of the time, Pallas kernels for 11%

profile of v2, /device:TPU:0, one launch (start us, length us, event | category | flops | bytes accessed | tf_op | source)
XLA Modules:
  0.0 20.4 jit_solution(18234275832600351120)
XLA Ops:
  0.6 0.0 copy-start.6
  0.6 0.9 %tail.1 = f32[128,128]{1,0:T(8,128)S(1)} custom-call(s32[48]{0:T(128)} %valid_hbm.3, f32[384,128]{1,0:T(8,128)} %bitcast.5), custom_call_target="tpu_custom_call" | custom-call | tf_op jit(solution)/shard_map/tail/pallas_call | solution.py:371
  1.6 4.9 %collective-permute-start = (f32[128,128]{1,0:T(8,128)S(1)}, f32[128,128]{1,0:T(8,128)S(1)}, u32[]{:S(2)}, u32[]{:S(2)}) collective-permute-start(f32[128,128]{1,0:T(8,128)S(1)} %tail.1), channel_id=1, source_target_pairs={{0,4},{4,8},{8,12},{12,16},{16,20},{20,24},{24,28},{1,5},{5,9},{9,... | collective-permute-start | bytes 196616 | tf_op jit(solution)/shard_map/ppermute | solution.py:384
  6.5 0.0 copy-done.6
  6.5 0.2 reshape.34.tmpl_ref
  6.6 0.0 copy-start
  6.7 0.0 copy-start.1
  6.7 0.0 copy-start.2
  6.7 0.0 copy-start.3
  6.7 0.0 copy-start.4
  6.7 0.0 copy-start.5
  6.7 2.2 %early.1 = (f32[512,256]{1,0:T(8,128)S(1)}, f32[2,2,256,256]{3,2,1,0:T(8,128)S(1)}, f32[8,128]{1,0:T(8,128)S(1)}) custom-call(s32[2]{0:T(128)} %len_hbm.1, f32[2]{0:T(128)} %weight_hbm.1, f32[2]{0:T(128)} %chirp_hbm.1, s32[48]{0:T(128)} %valid_hbm.3, f32[384,128]{1,0:T(8,128)} %bitcast.6, f32[256,128]{1,0:T(8,128)} %bitcast.7, ...), custom_call_target="tpu_custom_call" | custom-call | flops 2000000000 | bytes 2000000 | tf_op jit(solution)/shard_map/early/pallas_call | solution.py:385
  8.9 0.0 collective-permute-done.tail_ref
  8.9 0.0 copy-done
  9.0 0.0 copy-done.1
  9.0 0.0 copy-done.2
  9.0 0.0 copy-done.3
  9.0 0.0 copy-done.4
  9.0 0.0 copy-done.5
  9.0 3.6 %main.1 = (f32[200,128]{1,0:T(8,128)S(1)}, f32[200,128]{1,0:T(8,128)S(1)}, f32[200,128]{1,0:T(8,128)S(1)}, f32[200,128]{1,0:T(8,128)S(1)}) custom-call(f32[128,128]{1,0:T(8,128)S(1)} %collective-permute-done.tail_ref, f32[512,256]{1,0:T(8,128)S(1)} %get-tuple-element.13.section_ref, f32[2,2,256,256]{3,2,1,0:T(8,128)S(1)} %get-tuple-element.14.bank_ref, ...), custom_call_target="tpu_custom_call" | custom-call | flops 4000000000 | bytes 4000000 | tf_op jit(solution)/shard_map/main/pallas_call | solution.py:420
  12.6 0.1 collective-permute-start.1
  12.7 1.6 %collective-permute-start.2 = (f32[200,128]{1,0:T(8,128)S(1)}, f32[200,128]{1,0:T(8,128)S(1)}, u32[]{:S(2)}, u32[]{:S(2)}) collective-permute-start(f32[200,128]{1,0:T(8,128)S(1)} %get-tuple-element.18), channel_id=1, source_target_pairs={{0,2},{1,3},{2,0},{3,1},{4,6},{5,7},{6,4},{7,5},{8,10},{9,11},{10,... | collective-permute-start | bytes 307208 | tf_op jit(solution)/shard_map/ppermute | solution.py:437
  14.3 0.3 %collective-permute-start.3 = (f32[200,128]{1,0:T(8,128)S(1)}, f32[200,128]{1,0:T(8,128)S(1)}, u32[]{:S(2)}, u32[]{:S(2)}) collective-permute-start(f32[200,128]{1,0:T(8,128)S(1)} %get-tuple-element.19), channel_id=1, source_target_pairs={{0,3},{1,2},{2,1},{3,0},{4,7},{5,6},{6,5},{7,4},{8,11},{9,10},{10,... | collective-permute-start | bytes 307208 | tf_op jit(solution)/shard_map/ppermute | solution.py:437
  14.5 0.0 collective-permute-done.1.refs_1_
  14.6 4.0 %collective-permute-done.2.refs_2_ = f32[200,128]{1,0:T(8,128)S(1)} collective-permute-done((f32[200,128]{1,0:T(8,128)S(1)}, f32[200,128]{1,0:T(8,128)S(1)}, u32[]{:S(2)}, u32[]{:S(2)}) %collective-permute-start.2) | collective-permute-done | bytes 102432 | tf_op jit(solution)/shard_map/ppermute | solution.py:437
  18.5 1.1 %collective-permute-done.3.refs_3_ = f32[200,128]{1,0:T(8,128)S(1)} collective-permute-done((f32[200,128]{1,0:T(8,128)S(1)}, f32[200,128]{1,0:T(8,128)S(1)}, u32[]{:S(2)}, u32[]{:S(2)}) %collective-permute-start.3) | collective-permute-done | bytes 102432 | tf_op jit(solution)/shard_map/ppermute | solution.py:437
  19.6 0.8 %final.1 = (f32[96,128]{1,0:T(8,128)}, f32[96,128]{1,0:T(8,128)}, f32[96,128]{1,0:T(8,128)}) custom-call(f32[200,128]{1,0:T(8,128)S(1)} %get-tuple-element.16.refs_0_, f32[200,128]{1,0:T(8,128)S(1)} %collective-permute-done.1.refs_1_, f32[200,128]{1,0:T(8,128)S(1)} %collective-permute-done.2.refs_2_, f32[200,128]{1,0:T(8,128)S(1)} %collective-permute-done.3.refs_3_), custom_call_target="tpu_custom_call" | custom-call | tf_op jit(solution)/shard_map/final/pallas_call | solution.py:439
Async XLA Ops:
  0.6 5.8 %copy-start.6 = (bf16[2,2,32768]{2,1,0:T(2,128)(2,1)S(1)}, bf16[2,2,32768]{2,1,0:T(2,128)(2,1)}, u32[]{:S(2)}) copy-start(bf16[2,2,32768]{2,1,0:T(2,128)(2,1)} %param.16) | copy-start | bytes 786436
  1.6 7.4 %collective-permute-start = (f32[128,128]{1,0:T(8,128)S(1)}, f32[128,128]{1,0:T(8,128)S(1)}, u32[]{:S(2)}, u32[]{:S(2)}) collective-permute-start(f32[128,128]{1,0:T(8,128)S(1)} %tail.1), channel_id=1, source_target_pairs={{0,4},{4,8},{8,12},{12,16},{16,20},{20,24},{24,28},{1,5},{5,9},{9,... | collective-permute-start | bytes 196616 | tf_op jit(solution)/shard_map/ppermute | solution.py:384
  6.6 2.3 %copy-start = (bf16[3,512,256]{2,1,0:T(8,128)(2,1)S(1)}, bf16[3,512,256]{2,1,0:T(8,128)(2,1)}, u32[]{:S(2)}) copy-start(bf16[3,512,256]{2,1,0:T(8,128)(2,1)} %constant.16.clone.second_ref) | copy-start | bytes 2359300
  6.7 2.3 %copy-start.1 = (f32[2,256,256]{2,1,0:T(8,128)S(1)}, f32[2,256,256]{2,1,0:T(8,128)}, u32[]{:S(2)}) copy-start(f32[2,256,256]{2,1,0:T(8,128)} %constant.19.clone.twist_ref) | copy-start | bytes 1572868
  6.7 2.3 %copy-start.2 = (bf16[512,384]{1,0:T(8,128)(2,1)S(1)}, bf16[512,384]{1,0:T(8,128)(2,1)}, u32[]{:S(2)}) copy-start(bf16[512,384]{1,0:T(8,128)(2,1)} %constant.15.clone.head_ref) | copy-start | bytes 1179652
  6.7 2.3 %copy-start.3 = (bf16[2,3,128,256]{3,2,1,0:T(8,128)(2,1)S(1)}, bf16[2,3,128,256]{3,2,1,0:T(8,128)(2,1)}, u32[]{:S(2)}) copy-start(bf16[2,3,128,256]{3,2,1,0:T(8,128)(2,1)} %constant.17.clone.third_ref) | copy-start | bytes 1179652
  6.7 2.3 %copy-start.4 = (bf16[3,192,256]{2,1,0:T(8,128)(2,1)S(1)}, bf16[3,192,256]{2,1,0:T(8,128)(2,1)}, u32[]{:S(2)}) copy-start(bf16[3,192,256]{2,1,0:T(8,128)(2,1)} %constant.18.clone.fourth_ref) | copy-start | bytes 884740
  6.7 2.3 %copy-start.5 = (f32[2,128,128]{2,1,0:T(8,128)S(1)}, f32[2,128,128]{2,1,0:T(8,128)}, u32[]{:S(2)}) copy-start(f32[2,128,128]{2,1,0:T(8,128)} %constant.20.clone.turn_ref) | copy-start | bytes 393220
  12.6 1.9 %collective-permute-start.1 = (f32[200,128]{1,0:T(8,128)S(1)}, f32[200,128]{1,0:T(8,128)S(1)}, u32[]{:S(2)}, u32[]{:S(2)}) collective-permute-start(f32[200,128]{1,0:T(8,128)S(1)} %get-tuple-element.17), channel_id=1, source_target_pairs={{0,1},{1,0},{2,3},{3,2},{4,5},{5,4},{6,7},{7,6},{8,9},{9,8},{10,11... | collective-permute-start | bytes 307208 | tf_op jit(solution)/shard_map/ppermute | solution.py:437
  12.7 5.8 %collective-permute-start.2 = (f32[200,128]{1,0:T(8,128)S(1)}, f32[200,128]{1,0:T(8,128)S(1)}, u32[]{:S(2)}, u32[]{:S(2)}) collective-permute-start(f32[200,128]{1,0:T(8,128)S(1)} %get-tuple-element.18), channel_id=1, source_target_pairs={{0,2},{1,3},{2,0},{3,1},{4,6},{5,7},{6,4},{7,5},{8,10},{9,11},{10,... | collective-permute-start | bytes 307208 | tf_op jit(solution)/shard_map/ppermute | solution.py:437
  14.3 5.3 %collective-permute-start.3 = (f32[200,128]{1,0:T(8,128)S(1)}, f32[200,128]{1,0:T(8,128)S(1)}, u32[]{:S(2)}, u32[]{:S(2)}) collective-permute-start(f32[200,128]{1,0:T(8,128)S(1)} %get-tuple-element.19), channel_id=1, source_target_pairs={{0,3},{1,2},{2,1},{3,0},{4,7},{5,6},{6,5},{7,4},{8,11},{9,10},{10,... | collective-permute-start | bytes 307208 | tf_op jit(solution)/shard_map/ppermute | solution.py:437

commit v3 on v2

v3 whole, which is shorter than its diff:
```python
import functools
import math

import jax
import jax.numpy as jnp
import numpy as np
from jax import lax
from jax.experimental import pallas as pl
from jax.experimental.pallas import tpu as pltpu
from jax.sharding import PartitionSpec as P

NFFT = 65536
FA = 256
HALF = 128
OVER = 16384
RATE = 4096
LANES = 128
F32 = jnp.float32
BF16 = jnp.bfloat16

TERMS = ((0, 0), (0, 1), (1, 0), (1, 1), (0, 2), (2, 0))
FEW = TERMS[:3]
PARTS = 1 + max(max(term) for term in TERMS)


def parts_of_table(table):
    rest = np.asarray(table, np.float32)
    parts = []
    for _ in range(PARTS):
        part = rest.astype(jnp.bfloat16)
        parts.append(part)
        rest = rest - part.astype(np.float32)
    return parts


def complex_rows(angle, sign):
    cos, sin = np.cos(angle), sign * np.sin(angle)
    return np.block([[cos, -sin], [sin, cos]])


def padded(rows):
    return (rows + 7) // 8 * 8


@functools.cache
def tables(hop_rows, parts_out):
    index = np.arange(FA)
    grid = index[:, None] * index[None, :]
    full = 2.0 * math.pi / FA
    first = parts_of_table(np.concatenate([np.cos(grid % FA * full), -np.sin(grid % FA * full)]))
    rows = OVER // FA
    head = np.concatenate([first[i][:, :rows] for i, _ in TERMS], axis=1)
    quarter = np.arange(FA // 4)
    second = np.concatenate(
        [
            complex_rows((2 * quarter[:, None] + odd) * index[None, :] % FA * full, -1.0).T
            for odd in range(2)
        ],
        axis=1,
    )
    second = np.concatenate([part for part in parts_of_table(second)])
    third = []
    for odd in range(2):
        angle = index[:HALF, None] * (2 * quarter[None, :] + odd) % FA * full
        parts = parts_of_table(complex_rows(angle, 1.0).T)
        third.append(np.stack(parts))
    own = hop_rows // parts_out // 2
    fourth = []
    for dest in range(parts_out):
        angle = (dest * own + np.arange(own))[:, None] * index[None, :HALF] % HALF * (2.0 * full)
        block = complex_rows(angle, 1.0).reshape(2, own, FA)
        block = np.pad(block, ((0, 0), (0, padded(own) - own), (0, 0))).reshape(-1, FA)
        fourth.append(np.stack(parts_of_table(block)[:2]))
    fine = grid * (2.0 * math.pi / NFFT)
    turn = np.repeat(index[:HALF, None] * full, LANES, axis=1)
    return {
        "first": np.stack(first),
        "head": head,
        "second": second.reshape(PARTS, 2 * FA, FA),
        "third": np.stack(third),
        "fourth": np.stack(fourth),
        "twist": np.stack([np.cos(fine), np.sin(fine)]).astype(np.float32),
        "turn": np.stack([np.cos(turn), np.sin(turn)]).astype(np.float32),
    }


def split(value, count=PARTS):
    parts = []
    for step in range(count):
        part = value.astype(BF16)
        parts.append(part)
        if step < count - 1:
            value = value - part.astype(F32)
    return parts


def dot(left, right):
    return lax.dot_general(left, right, (((1,), (0,)), ((), ())), preferred_element_type=F32)


def left_terms(parts, terms=TERMS):
    return jnp.concatenate([parts[i] for i, _ in terms], axis=1)


def right_terms(parts, terms=TERMS):
    return jnp.concatenate([parts[j] for _, j in terms], axis=0)


def log_bessel(power):
    inv = lax.rsqrt(jnp.maximum(power, 1e-30))
    rho = power * inv
    small = rho < 3.75
    t = jnp.minimum(power, 3.75 * 3.75) * (1.0 / (3.75 * 3.75))
    small_poly = 1.0 + t * (
        3.5156229
        + t * (3.0899424 + t * (1.2067492 + t * (0.2659732 + t * (0.0360768 + t * 0.0045813))))
    )
    q = jnp.minimum(3.75 * inv, 1.0)
    large_poly = 0.39894228 + q * (
        0.01328592
        + q
        * (
            0.00225319
            + q
            * (
                -0.00157565
                + q
                * (
                    0.00916281
                    + q
                    * (-0.02057706 + q * (0.02635537 + q * (-0.01647633 + q * 0.00392377)))
                )
            )
        )
    )
    inner = jnp.where(small, small_poly, large_poly * lax.rsqrt(jnp.maximum(rho, 3.75)))
    return jnp.where(small, 0.0, rho) + jnp.log(inner)


def phase(index, period):
    wrapped = ((index + period // 2) & (period - 1)) - period // 2
    angle = wrapped.astype(F32) * (2.0 * math.pi / period)
    return jnp.cos(angle), jnp.sin(angle)


def frame_of(samples):
    rows = samples.shape[0] // 2
    return jnp.concatenate([samples[pl.ds(h, rows, stride=2), :] for h in range(2)], axis=1)


def tail_kernel(
    len_hbm,
    weight_hbm,
    chirp_hbm,
    valid_hbm,
    strain_hbm,
    out_ref,
    traits_ref,
    gates_ref,
    lens,
    weights,
    chirps,
    flags,
    samples,
    sems,
):
    rows = samples.shape[0]
    blocks = flags.shape[0]
    last = strain_hbm.at[pl.ds(strain_hbm.shape[0] - rows, rows), :]
    pairs = ((last, samples), (valid_hbm, flags), (len_hbm, lens), (weight_hbm, weights), (chirp_hbm, chirps))
    copies = [pltpu.make_async_copy(a, b, sems.at[i]) for i, (a, b) in enumerate(pairs)]
    for copy in copies:
        copy.start()
    for copy in copies:
        copy.wait()
    for i in range(rows // 8):
        here = slice(8 * i, 8 * i + 8)
        out_ref[here, :] = samples[here, :] * flags[blocks - rows // 8 + i].astype(F32)
    for i in range(blocks):
        gates_ref[i : i + 1, :] = jnp.full((1, LANES), flags[i].astype(F32))
    traits_ref[...] = traits_tile(lens, weights, chirps, lens.shape[0])


def bank_kernel(traits_ref, asd_ref, tmpl_ref, bank_ref):
    count = tmpl_ref.shape[1]
    bank_ref[2 * count * FA :, :] = traits_ref[...]
    lane = lax.broadcasted_iota(jnp.int32, (1, LANES), 1)
    quarter = FA // 4
    sign = jnp.where(lane < quarter, 1.0, -1.0)
    blocks = [(q, h) for q in range(2) for h in range(2)]
    asd = {(q, h): asd_ref[pl.ds(2 * q + h, quarter, stride=4), :] for q, h in blocks}
    for k in range(count):
        delay = traits_ref[3 * k + 2 : 3 * k + 3, :LANES]
        start = OVER - (delay * RATE).astype(jnp.int32)
        energy = jnp.zeros((1, 1), F32)
        turned = {}
        for q, h in blocks:
            re = tmpl_ref[0, k, pl.ds(2 * q + h, quarter, stride=4), :] * asd[q, h]
            im = tmpl_ref[1, k, pl.ds(2 * q + h, quarter, stride=4), :] * asd[q, h]
            energy += jnp.sum(re * re + im * im, keepdims=True)
            row_cos, row_sin = phase((lane + h * LANES) * start, NFFT)
            new_re = re * row_cos + im * row_sin
            new_im = re * row_sin - im * row_cos
            turned[q, h] = (
                jnp.concatenate([new_re, new_re], axis=0).T,
                jnp.concatenate([-new_im, new_im], axis=0).T,
            )
        scale = lax.rsqrt(energy) * (1.0 / math.sqrt(NFFT))
        for q in range(2):
            col_cos, col_sin = phase((2 * (lane & (quarter - 1)) + q) * start, FA)
            col_cos, col_sin = col_cos * scale, col_sin * sign * scale
            for h in range(2):
                own, cross = turned[q, h]
                cols = slice(q * LANES, q * LANES + LANES)
                for form, value in enumerate(
                    (own * col_cos + cross * col_sin, cross * col_cos - own * col_sin)
                ):
                    first = (2 * k + form) * FA + h * HALF
                    bank_ref[first : first + HALF, cols] = value


def section_kernel(gates_ref, strain_ref, first_ref, section_ref, gated):
    for i in range(gates_ref.shape[0]):
        here = slice(8 * i, 8 * i + 8)
        gated[here, :] = strain_ref[here, :] * gates_ref[i : i + 1, :]
    frame = frame_of(gated)
    pad = jnp.zeros((FA - frame.shape[0], FA), BF16)
    frame_parts = [jnp.concatenate([pad, part], axis=0) for part in split(frame)]
    section_ref[...] = dot(left_terms([first_ref[p] for p in range(PARTS)]), right_terms(frame_parts))


def spectrum_kernel(tail_ref, section_ref, head_ref, second_ref, twist_ref, spec_ref):
    section = section_ref[...] + dot(head_ref[...], right_terms(split(frame_of(tail_ref))))
    re, im = section[:FA], section[FA:]
    turn_cos, turn_sin = twist_ref[0], twist_ref[1]
    turned = jnp.concatenate([re * turn_cos + im * turn_sin, im * turn_cos - re * turn_sin], axis=1)
    spec = dot(left_terms(split(turned)), right_terms([second_ref[p] for p in range(PARTS)]))
    spec_ref[0] = spec
    spec_ref[1] = swapped(spec)


def swapped(value):
    return jnp.concatenate(
        [pltpu.roll(value[:, i : i + LANES], LANES // 2, axis=1) for i in range(0, value.shape[1], LANES)],
        axis=1,
    )


def powers_of(spec_ref, bank_ref, k, third_ref, left, twist_ref, turn_ref):
    first = 2 * k * FA
    prod = spec_ref[0] * bank_ref[first : first + FA, :] + spec_ref[1] * bank_ref[first + FA : first + 2 * FA, :]
    even, odd = (
        dot(
            left_terms(split(prod[:, q * LANES : (q + 1) * LANES])),
            right_terms([third_ref[q, p] for p in range(PARTS)]),
        )
        for q in range(2)
    )
    plus, minus = even + odd, even - odd
    in_re = jnp.concatenate([plus[:, :HALF], minus[:, :HALF]], axis=1)
    in_im = jnp.concatenate([plus[:, HALF:], minus[:, HALF:]], axis=1)
    turn_cos, turn_sin = twist_ref[0], twist_ref[1]
    out_re = in_re * turn_cos - in_im * turn_sin
    out_im = in_re * turn_sin + in_im * turn_cos
    sum_re, sum_im = out_re[:HALF] + out_re[HALF:], out_im[:HALF] + out_im[HALF:]
    gap_re, gap_im = out_re[:HALF] - out_re[HALF:], out_im[:HALF] - out_im[HALF:]
    half_cos = jnp.concatenate([turn_ref[0]] * 2, axis=1)
    half_sin = jnp.concatenate([turn_ref[1]] * 2, axis=1)
    odd_re, odd_im = gap_re * half_cos - gap_im * half_sin, gap_re * half_sin + gap_im * half_cos
    return [
        dot(left, right_terms(split(jnp.concatenate(piece, axis=0), 2), FEW))
        for piece in ((sum_re, sum_im), (odd_re, odd_im))
    ]


def marginal(powers, traits):
    scores = [log_bessel(power) for power in powers]
    peak = functools.reduce(jnp.maximum, scores)
    masses = [weight * jnp.exp(score - peak) for score, (weight, _, _) in zip(scores, traits)]
    total = functools.reduce(jnp.add, masses)
    chirp = functools.reduce(jnp.add, [mass * trait[1] for mass, trait in zip(masses, traits)])
    delay = functools.reduce(jnp.add, [mass * trait[2] for mass, trait in zip(masses, traits)])
    inv = 1.0 / total
    return peak + jnp.log(total), chirp * inv, delay * inv


def traits_of(banks, count):
    return [
        tuple(bank[2 * count * FA + 3 * k + i : 2 * count * FA + 3 * k + i + 1, :] for i in range(3))
        for bank in banks
        for k in range(count)
    ]


def store_marginal(out_ref, powers, traits):
    rows = powers[0][0].shape[0]
    for q in range(2):
        for i, value in enumerate(marginal([power[q] for power in powers], traits)):
            first = (3 * q + i) * rows
            out_ref[first : first + rows, :] = value
    prior = functools.reduce(jnp.add, [trait[0] for trait in traits])
    out_ref[6 * rows :, :] = jnp.broadcast_to(prior, (8, FA))


def traits_tile(lens, weights, chirps, count):
    rows = trait_rows(count)
    row = lax.broadcasted_iota(jnp.int32, (rows, FA), 0)
    tile = jnp.zeros((rows, FA), F32)
    for k in range(count):
        tile = jnp.where(row == 3 * k, weights[k], tile)
        tile = jnp.where(row == 3 * k + 1, chirps[k], tile)
        tile = jnp.where(row == 3 * k + 2, lens[k].astype(F32) / RATE, tile)
    return tile


def trait_rows(count):
    return (3 * count + 7) // 8 * 8


def partner(me, r, n, group):
    return me ^ (r * group) if n & (n - 1) == 0 else (me + r * group) % n


def main_kernel(spec_ref, *refs, group):
    banks, (third_ref, fourth_ref, twist_ref, turn_ref, own_ref, *outs) = refs[:group], refs[group:]
    n = fourth_ref.shape[0]
    count = (banks[0].shape[0] - trait_rows(1)) // (2 * FA)
    me = lax.axis_index("bank")
    dests = [partner(me, r, n, group) for r in range(n // group)]
    block = fourth_ref.shape[2]
    left = left_terms(
        [jnp.concatenate([fourth_ref[dest, p] for dest in dests], axis=0) for p in range(2)], FEW
    )
    powers = []
    for bank in banks:
        for k in range(count):
            powers.append([])
            for corr in powers_of(spec_ref, bank, k, third_ref, left, twist_ref, turn_ref):
                powers[-1].append([])
                for r in range(len(dests)):
                    re = corr[r * block : r * block + block // 2]
                    im = corr[r * block + block // 2 : (r + 1) * block]
                    powers[-1][-1].append(re * re + im * im)
    traits = traits_of(banks, count)
    for r, out in enumerate(outs, 1):
        store_marginal(out, [[power[q][r] for q in range(2)] for power in powers], traits)
    for i, power in enumerate(powers):
        for q in range(2):
            own_ref[i, q] = power[q][0]


def own_kernel(power_ref, *refs):
    *banks, out_ref = refs
    powers = [[power_ref[i, q] for q in range(2)] for i in range(power_ref.shape[0])]
    store_marginal(out_ref, powers, traits_of(banks, power_ref.shape[0] // len(banks)))


def final_kernel(*refs):
    *sides, log_ref, chirp_ref, delay_ref = refs
    rows = (sides[0].shape[0] - 8) // 6
    keep = log_ref.shape[0] // 4
    prior = functools.reduce(jnp.add, [side[6 * rows : 6 * rows + 1, :] for side in sides])
    log_prior = jnp.log(prior)
    for q in range(2):
        logs, chirps, delays = (
            [side[(3 * q + i) * rows : (3 * q + i + 1) * rows, :] for side in sides] for i in range(3)
        )
        peak = functools.reduce(jnp.maximum, logs)
        masses = [jnp.exp(value - peak) for value in logs]
        total = functools.reduce(jnp.add, masses)
        inv = 1.0 / total
        chirp = functools.reduce(jnp.add, [m * value for m, value in zip(masses, chirps)]) * inv
        delay = functools.reduce(jnp.add, [m * value for m, value in zip(masses, delays)]) * inv
        level = peak + jnp.log(total) - log_prior
        for ref, value in ((log_ref, level), (chirp_ref, chirp), (delay_ref, delay)):
            for h in range(2):
                ref[pl.ds(2 * q + h, keep, stride=4), :] = value[:keep, h * LANES : (h + 1) * LANES]


HBM = pl.BlockSpec(memory_space=pltpu.HBM)
VMEM = pl.BlockSpec(memory_space=pltpu.VMEM)


def in_hbm(value):
    return pltpu.with_memory_space_constraint(value, pltpu.HBM)


def params(mib):
    return pltpu.CompilerParams(vmem_limit_bytes=mib * 1024 * 1024)


def steps(strain, inv_asd, templates, tmpl_len, weights, chirp_mass, valid):
    n = lax.axis_size("bank")
    segs = lax.axis_size("seg")
    count = templates.shape[1]
    rows = strain.shape[0] // LANES
    tail_rows = OVER // LANES
    flags = valid.shape[0]
    group = 2 if n % 2 == 0 else 1
    table = {key: jnp.asarray(value) for key, value in tables(rows // 2, n).items()}
    strain = strain.reshape(rows, LANES)
    asd = inv_asd.reshape(-1, LANES)
    tail, traits, gates = pl.pallas_call(
        tail_kernel,
        in_specs=[HBM] * 5,
        out_specs=[VMEM] * 3,
        out_shape=[
            pltpu.VMEM((tail_rows, LANES), F32),
            pltpu.VMEM((trait_rows(count), FA), F32),
            pltpu.VMEM((flags, LANES), F32),
        ],
        scratch_shapes=[
            pltpu.SMEM((count,), jnp.int32),
            pltpu.SMEM((count,), F32),
            pltpu.SMEM((count,), F32),
            pltpu.SMEM((flags,), jnp.int32),
            pltpu.VMEM((tail_rows, LANES), F32),
            pltpu.SemaphoreType.DMA((5,)),
        ],
        compiler_params=params(4),
        cost_estimate=pl.CostEstimate(flops=4 * 10**9, bytes_accessed=10**5, transcendentals=0),
        name="tail",
    )(*map(in_hbm, (tmpl_len, weights, chirp_mass, valid, strain)))
    halo = lax.ppermute(tail, "seg", [(i, i + 1) for i in range(segs - 1)])
    bank = pl.pallas_call(
        bank_kernel,
        in_specs=[VMEM] * 3,
        out_specs=VMEM,
        out_shape=pltpu.VMEM((2 * count * FA + trait_rows(count), FA), F32),
        compiler_params=params(8),
        cost_estimate=pl.CostEstimate(flops=10**6, bytes_accessed=10**4, transcendentals=0),
        name="bank",
    )(traits, asd, templates.astype(F32).reshape(2, count, -1, LANES))
    banks = [bank] + [
        lax.ppermute(bank, "bank", [(i, i // group * group + (i + r) % group) for i in range(n)])
        for r in range(1, group)
    ]
    section = pl.pallas_call(
        section_kernel,
        in_specs=[VMEM] * 3,
        out_specs=VMEM,
        out_shape=pltpu.VMEM((2 * FA, FA), F32),
        scratch_shapes=[pltpu.VMEM((rows, LANES), F32)],
        compiler_params=params(12),
        cost_estimate=pl.CostEstimate(flops=10**6, bytes_accessed=10**4, transcendentals=0),
        name="section",
    )(gates, strain, table["first"])
    spec = pl.pallas_call(
        spectrum_kernel,
        in_specs=[VMEM] * 5,
        out_specs=VMEM,
        out_shape=pltpu.VMEM((2, FA, FA), F32),
        compiler_params=params(10),
        cost_estimate=pl.CostEstimate(flops=10**6, bytes_accessed=10**4, transcendentals=0),
        name="spectrum",
    )(halo, section, table["head"], table["second"], table["twist"])
    own_rows = padded(rows // 4 // n)
    side = pltpu.VMEM((6 * own_rows + 8, FA), F32)
    powers, *outs = pl.pallas_call(
        functools.partial(main_kernel, group=group),
        in_specs=[VMEM] * (5 + group),
        out_specs=[VMEM] * (n // group),
        out_shape=[pltpu.VMEM((count * group, 2, own_rows, FA), F32)] + [side] * (n // group - 1),
        compiler_params=params(20),
        cost_estimate=pl.CostEstimate(flops=4 * 10**9, bytes_accessed=4 * 10**6, transcendentals=0),
        name="main",
    )(spec, *banks, *(table[key] for key in ("third", "fourth", "twist", "turn")))
    sides = [
        lax.ppermute(out, "bank", [(i, partner(i, r, n, group)) for i in range(n)])
        for r, out in enumerate(outs, 1)
    ]
    own = pl.pallas_call(
        own_kernel,
        in_specs=[VMEM] * (1 + group),
        out_specs=VMEM,
        out_shape=side,
        compiler_params=params(6),
        cost_estimate=pl.CostEstimate(flops=10**9, bytes_accessed=10**6, transcendentals=0),
        name="own",
    )(powers, *banks)
    results = pl.pallas_call(
        final_kernel,
        in_specs=[VMEM] * (n // group),
        out_specs=[VMEM] * 3,
        out_shape=[jax.ShapeDtypeStruct((rows // n, LANES), F32)] * 3,
        compiler_params=params(6),
        name="final",
    )(own, *sides)
    return tuple(result.reshape(-1) for result in results)


def solution(mesh):
    placed = (P("seg"), P(), P(None, "bank", None), P("bank"), P("bank"), P("bank"), P("seg"))
    return jax.shard_map(
        steps,
        mesh=mesh,
        in_specs=placed,
        out_specs=(P(("seg", "bank")), P(("seg", "bank")), P(("seg", "bank"))),
        check_vma=False,
    )
```

time: 20.8 us -> 20.9 us (level)
  the two profiles are of different devices: /device:TPU:0 before, /device:TPU:12 now
where the time goes in v3:
time: 20.9 us; the launch traced here: 20.8 us
  waiting for transfers between devices  7.62 us (36%)
  Pallas kernels  6.97 us (33%)
  starting transfers between devices  4.17 us (20%)
  local copies, waits for them, and re-layouts  1.18 us (6%)
  between operations  0.81 us (4%)
    ppermute x1, waiting for transfers between devices, steps(): lax.ppermute(out, 'bank', [(i, partner(i, r, n, group)) for i in range(n)])  4.54 us
    ppermute x1, starting transfers between devices, steps(): halo = lax.ppermute(tail, 'seg', [(i, i + 1) for i in range(segs - 1)])  3.53 us
    ppermute x1, waiting for transfers between devices, steps(): halo = lax.ppermute(tail, 'seg', [(i, i + 1) for i in range(segs - 1)])  3.07 us
    pallas_call x1, Pallas kernels, steps(): pl.pallas_call(functools.partial(main_kernel, group=group), in_specs=[VME...  2.66 us
    pallas_call x1, Pallas kernels, steps(): pl.pallas_call(spectrum_kernel, in_specs=[VMEM] * 5, out_specs=VMEM, out_...  1.17 us
    reshape x1, local copies, waits for them, and re-layouts, steps(): templates.astype(F32).reshape(2, count, -1, LANES)  1.12 us
    pallas_call x1, Pallas kernels, steps(): pl.pallas_call(tail_kernel, in_specs=[HBM] * 5, out_specs=[VMEM] * 3, out...  0.99 us
    pallas_call x1, Pallas kernels, steps(): pl.pallas_call(final_kernel, in_specs=[VMEM] * (n // group), out_specs=[V...  0.69 us
  transfers between devices with their start and end apart: 3, of which 2 were waited for; matrix products, arithmetic and copies ran while one was open for 0% of the time, Pallas kernels for 10%

profile of v3, /device:TPU:12, one launch (start us, length us, event | category | flops | bytes accessed | tf_op | source)
XLA Modules:
  0.0 20.8 jit_solution(12916032201369618816)
XLA Ops:
  0.6 1.1 %reshape.34.tmpl_ref = f32[2,2,256,128]{3,2,1,0:T(8,128)S(1)} reshape(bf16[2,2,32768]{2,1,0:T(2,128)(2,1)} %param.16) | data formatting | bytes 786432 | tf_op jit(solution)/shard_map/reshape | solution.py:433
  1.8 0.0 copy-start.5
  1.8 1.0 %tail.1 = (f32[128,128]{1,0:T(8,128)S(1)}, f32[8,256]{1,0:T(8,128)S(1)}, f32[48,128]{1,0:T(8,128)S(1)}) custom-call(s32[2]{0:T(128)} %len_hbm.1, f32[2]{0:T(128)} %weight_hbm.1, f32[2]{0:T(128)} %chirp_hbm.1, s32[48]{0:T(128)} %valid_hbm.1, f32[384,128]{1,0:T(8,128)} %bitcast.5), custom_call_target="tpu_custom_call" | custom-call | flops 4000000000 | bytes 100000 | tf_op jit(solution)/shard_map/tail/pallas_call | solution.py:403
  2.8 0.0 copy-start
  2.8 0.0 copy-start.4
  2.8 0.0 copy-done.5
  2.8 0.0 copy-start.3
  2.8 0.5 %bank.1.refs_0_ = f32[1032,256]{1,0:T(8,128)S(1)} custom-call(f32[8,256]{1,0:T(8,128)S(1)} %get-tuple-element.13.traits_ref, f32[256,128]{1,0:T(8,128)S(1)} %bitcast.7, f32[2,2,256,128]{3,2,1,0:T(8,128)S(1)} %reshape.34.tmpl_ref), custom_call_target="tpu_custom_call" | custom-call | flops 1000000 | bytes 10000 | tf_op jit(solution)/shard_map/bank/pallas_call | solution.py:425
  3.3 0.0 copy-start.1
  3.3 0.0 copy-start.2
  3.3 0.1 collective-permute-start.1
  3.4 3.5 %collective-permute-start = (f32[128,128]{1,0:T(8,128)S(1)}, f32[128,128]{1,0:T(8,128)S(1)}, u32[]{:S(2)}, u32[]{:S(2)}) collective-permute-start(f32[128,128]{1,0:T(8,128)S(1)} %get-tuple-element.11), channel_id=1, source_target_pairs={{0,4},{4,8},{8,12},{12,16},{16,20},{20,24},{24,28},{1,5},{5,9},{9,... | collective-permute-start | bytes 196616 | tf_op jit(solution)/shard_map/ppermute | solution.py:424
  7.0 0.0 copy-done
  7.0 0.0 copy-done.4
  7.0 0.6 %section.1.section_ref = f32[512,256]{1,0:T(8,128)S(1)} custom-call(f32[48,128]{1,0:T(8,128)S(1)} %get-tuple-element.12.gates_ref, f32[384,128]{1,0:T(8,128)S(1)} %bitcast.6, bf16[3,512,256]{2,1,0:T(8,128)(2,1)S(1)} %copy-done), custom_call_target="tpu_custom_call" | custom-call | flops 1000000 | bytes 10000 | tf_op jit(solution)/shard_map/section/pallas_call | solution.py:438
  7.6 0.0 copy-start.6
  7.6 0.0 copy-start.7
  7.6 0.0 copy-start.8
  7.6 3.1 %collective-permute-done.tail_ref = f32[128,128]{1,0:T(8,128)S(1)} collective-permute-done((f32[128,128]{1,0:T(8,128)S(1)}, f32[128,128]{1,0:T(8,128)S(1)}, u32[]{:S(2)}, u32[]{:S(2)}) %collective-permute-start) | collective-permute-done | bytes 65568 | tf_op jit(solution)/shard_map/ppermute | solution.py:424
  10.7 0.0 copy-done.3
  10.7 0.0 copy-done.1
  10.7 0.0 copy-done.2
  10.7 1.2 %spectrum.1.spec_ref = f32[2,256,256]{2,1,0:T(8,128)S(1)} custom-call(f32[128,128]{1,0:T(8,128)S(1)} %collective-permute-done.tail_ref, f32[512,256]{1,0:T(8,128)S(1)} %section.1.section_ref, bf16[512,384]{1,0:T(8,128)(2,1)S(1)} %copy-done.3, bf16[3,512,256]{2,1,0:T(8,128)(2,1)S(1)} %copy-done.1, f32[2,256,256]{2,1,0:T(8,128)S(1)} %copy-done.2), custom_call_target="tpu_custom_call" | custom-call | flops 1000000 | bytes 10000 | tf_op jit(solution)/shard_map/spectrum/pallas_call | solution.py:448
  11.9 0.0 collective-permute-done.1.refs_1_
  11.9 0.0 copy-done.6
  11.9 0.0 copy-done.7
  11.9 0.0 copy-done.8
  11.9 2.7 %main.1 = (f32[4,2,24,256]{3,2,1,0:T(8,128)S(1)}, f32[152,256]{1,0:T(8,128)S(1)}) custom-call(f32[2,256,256]{2,1,0:T(8,128)S(1)} %spectrum.1.spec_ref, f32[1032,256]{1,0:T(8,128)S(1)} %bank.1.refs_0_, f32[1032,256]{1,0:T(8,128)S(1)} %collective-permute-done.1.refs_1_, bf16[2,3,128,256]{3,2,1,0:T(8,128)(2,1)S(1)} %copy-done.6, ...), custom_call_target="tpu_custom_call" | custom-call | flops 4000000000 | bytes 4000000 | tf_op jit(solution)/shard_map/main/pallas_call | solution.py:459
  14.6 0.6 %collective-permute-start.2 = (f32[152,256]{1,0:T(8,128)S(1)}, f32[152,256]{1,0:T(8,128)S(1)}, u32[]{:S(2)}, u32[]{:S(2)}) collective-permute-start(f32[152,256]{1,0:T(8,128)S(1)} %get-tuple-element.15), channel_id=1, source_target_pairs={{0,2},{1,3},{2,0},{3,1},{4,6},{5,7},{6,4},{7,5},{8,10},{9,11},{10,... | collective-permute-start | bytes 466952 | tf_op jit(solution)/shard_map/ppermute | solution.py:469
  15.2 0.4 %own.1.refs_0_ = f32[152,256]{1,0:T(8,128)S(1)} custom-call(f32[4,2,24,256]{3,2,1,0:T(8,128)S(1)} %get-tuple-element.14.power_ref, f32[1032,256]{1,0:T(8,128)S(1)} %bank.1.refs_0_, f32[1032,256]{1,0:T(8,128)S(1)} %collective-permute-done.1.refs_1_), custom_call_target="tpu_custom_call" | custom-call | flops 1000000000 | bytes 1000000 | tf_op jit(solution)/shard_map/own/pallas_call | solution.py:472
  15.5 4.5 %collective-permute-done.2.refs_1_ = f32[152,256]{1,0:T(8,128)S(1)} collective-permute-done((f32[152,256]{1,0:T(8,128)S(1)}, f32[152,256]{1,0:T(8,128)S(1)}, u32[]{:S(2)}, u32[]{:S(2)}) %collective-permute-start.2) | collective-permute-done | bytes 155680 | tf_op jit(solution)/shard_map/ppermute | solution.py:469
  20.1 0.7 %final.1 = (f32[96,128]{1,0:T(8,128)}, f32[96,128]{1,0:T(8,128)}, f32[96,128]{1,0:T(8,128)}) custom-call(f32[152,256]{1,0:T(8,128)S(1)} %own.1.refs_0_, f32[152,256]{1,0:T(8,128)S(1)} %collective-permute-done.2.refs_1_), custom_call_target="tpu_custom_call" | custom-call | tf_op jit(solution)/shard_map/final/pallas_call | solution.py:481
Async XLA Ops:
  1.8 1.0 %copy-start.5 = (f32[32768]{0:T(1024)S(1)}, f32[32768]{0:T(1024)}, u32[]{:S(2)}) copy-start(f32[32768]{0:T(1024)} %param.15) | copy-start | bytes 393220
  2.8 4.2 %copy-start = (bf16[3,512,256]{2,1,0:T(8,128)(2,1)S(1)}, bf16[3,512,256]{2,1,0:T(8,128)(2,1)}, u32[]{:S(2)}) copy-start(bf16[3,512,256]{2,1,0:T(8,128)(2,1)} %constant.14.clone.first_ref) | copy-start | bytes 2359300
  2.8 4.2 %copy-start.4 = (f32[49152]{0:T(1024)S(1)}, f32[49152]{0:T(1024)}, u32[]{:S(2)}) copy-start(f32[49152]{0:T(1024)} %param.14) | copy-start | bytes 589828
  2.8 7.9 %copy-start.3 = (bf16[512,384]{1,0:T(8,128)(2,1)S(1)}, bf16[512,384]{1,0:T(8,128)(2,1)}, u32[]{:S(2)}) copy-start(bf16[512,384]{1,0:T(8,128)(2,1)} %constant.15.clone.head_ref) | copy-start | bytes 1179652
  3.3 7.4 %copy-start.1 = (bf16[3,512,256]{2,1,0:T(8,128)(2,1)S(1)}, bf16[3,512,256]{2,1,0:T(8,128)(2,1)}, u32[]{:S(2)}) copy-start(bf16[3,512,256]{2,1,0:T(8,128)(2,1)} %constant.16.clone.second_ref) | copy-start | bytes 2359300
  3.3 7.4 %copy-start.2 = (f32[2,256,256]{2,1,0:T(8,128)S(1)}, f32[2,256,256]{2,1,0:T(8,128)}, u32[]{:S(2)}) copy-start(f32[2,256,256]{2,1,0:T(8,128)} %constant.19.clone.twist_ref.refs_4_) | copy-start | bytes 1572868
  3.3 8.5 %collective-permute-start.1 = (f32[1032,256]{1,0:T(8,128)S(1)}, f32[1032,256]{1,0:T(8,128)S(1)}, u32[]{:S(2)}, u32[]{:S(2)}) collective-permute-start(f32[1032,256]{1,0:T(8,128)S(1)} %bank.1.refs_0_), channel_id=1, source_target_pairs={{0,1},{1,0},{2,3},{3,2},{4,5},{5,4},{6,7},{7,6},{8,9},{9,8},{10,11... | collective-permute-start | bytes 3170312 | tf_op jit(solution)/shard_map/ppermute | solution.py:435
  3.4 7.3 %collective-permute-start = (f32[128,128]{1,0:T(8,128)S(1)}, f32[128,128]{1,0:T(8,128)S(1)}, u32[]{:S(2)}, u32[]{:S(2)}) collective-permute-start(f32[128,128]{1,0:T(8,128)S(1)} %get-tuple-element.11), channel_id=1, source_target_pairs={{0,4},{4,8},{8,12},{12,16},{16,20},{20,24},{24,28},{1,5},{5,9},{9,... | collective-permute-start | bytes 196616 | tf_op jit(solution)/shard_map/ppermute | solution.py:424
  7.6 4.3 %copy-start.6 = (bf16[2,3,128,256]{3,2,1,0:T(8,128)(2,1)S(1)}, bf16[2,3,128,256]{3,2,1,0:T(8,128)(2,1)}, u32[]{:S(2)}) copy-start(bf16[2,3,128,256]{3,2,1,0:T(8,128)(2,1)} %constant.17.clone.refs_2_) | copy-start | bytes 1179652
  7.6 4.3 %copy-start.7 = (bf16[4,2,48,256]{3,2,1,0:T(8,128)(2,1)S(1)}, bf16[4,2,48,256]{3,2,1,0:T(8,128)(2,1)}, u32[]{:S(2)}) copy-start(bf16[4,2,48,256]{3,2,1,0:T(8,128)(2,1)} %constant.18.clone.refs_3_) | copy-start | bytes 589828
  7.6 4.3 %copy-start.8 = (f32[2,128,128]{2,1,0:T(8,128)S(1)}, f32[2,128,128]{2,1,0:T(8,128)}, u32[]{:S(2)}) copy-start(f32[2,128,128]{2,1,0:T(8,128)} %constant.20.clone.refs_5_) | copy-start | bytes 393220
  14.6 5.5 %collective-permute-start.2 = (f32[152,256]{1,0:T(8,128)S(1)}, f32[152,256]{1,0:T(8,128)S(1)}, u32[]{:S(2)}, u32[]{:S(2)}) collective-permute-start(f32[152,256]{1,0:T(8,128)S(1)} %get-tuple-element.15), channel_id=1, source_target_pairs={{0,2},{1,3},{2,0},{3,1},{4,6},{5,7},{6,4},{7,5},{8,10},{9,11},{10,... | collective-permute-start | bytes 466952 | tf_op jit(solution)/shard_map/ppermute | solution.py:469

commit v4 on v3

--- a/solution.py
+++ b/solution.py
@@ -229,8 +229,14 @@
     section_ref[...] = dot(left_terms([first_ref[p] for p in range(PARTS)]), right_terms(frame_parts))
 
 
-def spectrum_kernel(tail_ref, section_ref, head_ref, second_ref, twist_ref, spec_ref):
-    section = section_ref[...] + dot(head_ref[...], right_terms(split(frame_of(tail_ref))))
+def spectrum_kernel(section_ref, head_ref, second_ref, twist_ref, *refs, segs):
+    *halos, spec_ref = refs
+    seg = lax.axis_index("seg")
+    halo = frame_of(halos[0])
+    if len(halos) > 1:
+        halo = jnp.where(seg == segs // 2 - 1, frame_of(halos[1]), halo)
+    halo = jnp.where(seg == 0, 0.0, halo)
+    section = section_ref[...] + dot(head_ref[...], right_terms(split(halo)))
     re, im = section[:FA], section[FA:]
     turn_cos, turn_sin = twist_ref[0], twist_ref[1]
     turned = jnp.concatenate([re * turn_cos + im * turn_sin, im * turn_cos - re * turn_sin], axis=1)
@@ -387,6 +393,20 @@
 
 def params(mib):
     return pltpu.CompilerParams(vmem_limit_bytes=mib * 1024 * 1024)
+
+
+def halo_routes(segs, n):
+    cut = segs // 2 - 1
+    if n % 2 or cut < 2:
+        return [(i, i + 1) for i in range(segs - 1)], []
+    closing = {cut - 1: 0, segs - 1: cut}
+    ring = [(i, closing.get(i, i + 1)) for i in range(segs)]
+    bridge = []
+    for i in range(segs):
+        for j in range(n):
+            to = (2 * cut - 1 - i) * n + j if i in (cut - 1, cut) else i * n + (j ^ 1)
+            bridge.append((i * n + j, to))
+    return ring, bridge
 
 
 def steps(strain, inv_asd, templates, tmpl_len, weights, chirp_mass, valid):
@@ -421,7 +441,10 @@
         cost_estimate=pl.CostEstimate(flops=4 * 10**9, bytes_accessed=10**5, transcendentals=0),
         name="tail",
     )(*map(in_hbm, (tmpl_len, weights, chirp_mass, valid, strain)))
-    halo = lax.ppermute(tail, "seg", [(i, i + 1) for i in range(segs - 1)])
+    ring, bridge = halo_routes(segs, n)
+    halos = [lax.ppermute(tail, "seg", ring)]
+    if bridge:
+        halos.append(lax.ppermute(tail, ("seg", "bank"), bridge))
     bank = pl.pallas_call(
         bank_kernel,
         in_specs=[VMEM] * 3,
@@ -446,14 +469,14 @@
         name="section",
     )(gates, strain, table["first"])
     spec = pl.pallas_call(
-        spectrum_kernel,
-        in_specs=[VMEM] * 5,
+        functools.partial(spectrum_kernel, segs=segs),
+        in_specs=[VMEM] * (4 + len(halos)),
         out_specs=VMEM,
         out_shape=pltpu.VMEM((2, FA, FA), F32),
         compiler_params=params(10),
         cost_estimate=pl.CostEstimate(flops=10**6, bytes_accessed=10**4, transcendentals=0),
         name="spectrum",
-    )(halo, section, table["head"], table["second"], table["twist"])
+    )(section, table["head"], table["second"], table["twist"], *halos)
     own_rows = padded(rows // 4 // n)
     side = pltpu.VMEM((6 * own_rows + 8, FA), F32)
     powers, *outs = pl.pallas_call(

time: 20.9 us -> 20.8 us (level)
  the two profiles are of different devices: /device:TPU:12 before, /device:TPU:0 now
where the time goes in v4:
time: 20.8 us; the launch traced here: 20.6 us
  Pallas kernels  6.98 us (34%)
  waiting for transfers between devices  6.51 us (31%)
  starting transfers between devices  5.13 us (25%)
  local copies, waits for them, and re-layouts  1.18 us (6%)
  between operations  0.79 us (4%)
    ppermute x1, waiting for transfers between devices, steps(): lax.ppermute(out, 'bank', [(i, partner(i, r, n, group)) for i in range(n)])  3.62 us
    ppermute x1, starting transfers between devices, steps(): halos = [lax.ppermute(tail, 'seg', ring)]  2.91 us
    ppermute x1, waiting for transfers between devices, steps(): halos = [lax.ppermute(tail, 'seg', ring)]  2.89 us
    pallas_call x1, Pallas kernels, steps(): pl.pallas_call(functools.partial(main_kernel, group=group), in_specs=[VME...  2.66 us
    ppermute x1, starting transfers between devices, steps(): lax.ppermute(out, 'bank', [(i, partner(i, r, n, group)) for i in range(n)])  1.58 us
    pallas_call x1, Pallas kernels, steps(): pl.pallas_call(functools.partial(spectrum_kernel, segs=segs), in_specs=[V...  1.19 us
    reshape x1, local copies, waits for them, and re-layouts, steps(): templates.astype(F32).reshape(2, count, -1, LANES)  1.12 us
    pallas_call x1, Pallas kernels, steps(): pl.pallas_call(tail_kernel, in_specs=[HBM] * 5, out_specs=[VMEM] * 3, out...  0.99 us
  transfers between devices with their start and end apart: 4, of which 2 were waited for; matrix products, arithmetic and copies ran while one was open for 0% of the time, Pallas kernels for 10%

profile of v4, /device:TPU:0, one launch (start us, length us, event | category | flops | bytes accessed | tf_op | source)
XLA Modules:
  0.0 20.6 jit_solution(5293948294482878074)
XLA Ops:
  0.6 1.1 %reshape.34.tmpl_ref = f32[2,2,256,128]{3,2,1,0:T(8,128)S(1)} reshape(bf16[2,2,32768]{2,1,0:T(2,128)(2,1)} %param.16) | data formatting | bytes 786432 | tf_op jit(solution)/shard_map/reshape | solution.py:456
  1.8 0.0 copy-start.5
  1.8 1.0 %tail.1 = (f32[128,128]{1,0:T(8,128)S(1)}, f32[8,256]{1,0:T(8,128)S(1)}, f32[48,128]{1,0:T(8,128)S(1)}) custom-call(s32[2]{0:T(128)} %len_hbm.1, f32[2]{0:T(128)} %weight_hbm.1, f32[2]{0:T(128)} %chirp_hbm.1, s32[48]{0:T(128)} %valid_hbm.1, f32[384,128]{1,0:T(8,128)} %bitcast.5), custom_call_target="tpu_custom_call" | custom-call | flops 4000000000 | bytes 100000 | tf_op jit(solution)/shard_map/tail/pallas_call | solution.py:423
  2.8 0.0 copy-start
  2.8 0.0 copy-start.4
  2.8 0.0 copy-done.5
  2.8 0.0 copy-start.3
  2.8 0.5 %bank.1.refs_0_ = f32[1032,256]{1,0:T(8,128)S(1)} custom-call(f32[8,256]{1,0:T(8,128)S(1)} %get-tuple-element.13.traits_ref, f32[256,128]{1,0:T(8,128)S(1)} %bitcast.7, f32[2,2,256,128]{3,2,1,0:T(8,128)S(1)} %reshape.34.tmpl_ref), custom_call_target="tpu_custom_call" | custom-call | flops 1000000 | bytes 10000 | tf_op jit(solution)/shard_map/bank/pallas_call | solution.py:448
  3.3 0.0 copy-start.1
  3.3 0.0 copy-start.2
  3.3 0.6 %collective-permute-start.2 = (f32[1032,256]{1,0:T(8,128)S(1)}, f32[1032,256]{1,0:T(8,128)S(1)}, u32[]{:S(2)}, u32[]{:S(2)}) collective-permute-start(f32[1032,256]{1,0:T(8,128)S(1)} %bank.1.refs_0_), channel_id=1, source_target_pairs={{0,1},{1,0},{2,3},{3,2},{4,5},{5,4},{6,7},{7,6},{8,9},{9,8},{10,11... | collective-permute-start | bytes 3170312 | tf_op jit(solution)/shard_map/ppermute | solution.py:458
  3.9 0.1 collective-permute-start.1
  4.0 2.9 %collective-permute-start = (f32[128,128]{1,0:T(8,128)S(1)}, f32[128,128]{1,0:T(8,128)S(1)}, u32[]{:S(2)}, u32[]{:S(2)}) collective-permute-start(f32[128,128]{1,0:T(8,128)S(1)} %get-tuple-element.12), channel_id=1, source_target_pairs={{0,4},{4,8},{8,0},{12,16},{16,20},{20,24},{24,28},{28,12},{1,5},{5... | collective-permute-start | bytes 196616 | tf_op jit(solution)/shard_map/ppermute | solution.py:445
  6.9 0.0 copy-done
  6.9 0.0 copy-done.4
  6.9 0.6 %section.1.section_ref = f32[512,256]{1,0:T(8,128)S(1)} custom-call(f32[48,128]{1,0:T(8,128)S(1)} %get-tuple-element.11.gates_ref, f32[384,128]{1,0:T(8,128)S(1)} %bitcast.6, bf16[3,512,256]{2,1,0:T(8,128)(2,1)S(1)} %copy-done), custom_call_target="tpu_custom_call" | custom-call | flops 1000000 | bytes 10000 | tf_op jit(solution)/shard_map/section/pallas_call | solution.py:461
  7.5 0.0 copy-start.6
  7.5 0.0 copy-start.7
  7.5 0.0 copy-start.8
  7.5 0.0 collective-permute-done.1.refs_1_
  7.5 2.9 %collective-permute-done.refs_0_ = f32[128,128]{1,0:T(8,128)S(1)} collective-permute-done((f32[128,128]{1,0:T(8,128)S(1)}, f32[128,128]{1,0:T(8,128)S(1)}, u32[]{:S(2)}, u32[]{:S(2)}) %collective-permute-start) | collective-permute-done | bytes 65568 | tf_op jit(solution)/shard_map/ppermute | solution.py:445
  10.4 0.0 copy-done.3
  10.4 1.2 %spectrum.1.spec_ref = f32[2,256,256]{2,1,0:T(8,128)S(1)} custom-call(f32[512,256]{1,0:T(8,128)S(1)} %section.1.section_ref, bf16[512,384]{1,0:T(8,128)(2,1)S(1)} %copy-done.3, bf16[3,512,256]{2,1,0:T(8,128)(2,1)S(1)} %copy-done.1, f32[2,256,256]{2,1,0:T(8,128)S(1)} %copy-done.2, f32[128,128]{1,0:T(8,128)S(1)} %collective-permute-done.refs_0_, ...), custom_call_target="tpu_custom_call" | custom-call | flops 1000000 | bytes 10000 | tf_op jit(solution)/shard_map/spectrum/pallas_call | solution.py:471
  11.6 0.0 collective-permute-done.2.refs_1_
  11.6 0.0 copy-done.6
  11.6 0.0 copy-done.7
  11.7 0.0 copy-done.8
  11.7 2.7 %main.1 = (f32[4,2,24,256]{3,2,1,0:T(8,128)S(1)}, f32[152,256]{1,0:T(8,128)S(1)}) custom-call(f32[2,256,256]{2,1,0:T(8,128)S(1)} %spectrum.1.spec_ref, f32[1032,256]{1,0:T(8,128)S(1)} %bank.1.refs_0_, f32[1032,256]{1,0:T(8,128)S(1)} %collective-permute-done.2.refs_1_, bf16[2,3,128,256]{3,2,1,0:T(8,128)(2,1)S(1)} %copy-done.6, ...), custom_call_target="tpu_custom_call" | custom-call | flops 4000000000 | bytes 4000000 | tf_op jit(solution)/shard_map/main/pallas_call | solution.py:482
  14.3 1.6 %collective-permute-start.3 = (f32[152,256]{1,0:T(8,128)S(1)}, f32[152,256]{1,0:T(8,128)S(1)}, u32[]{:S(2)}, u32[]{:S(2)}) collective-permute-start(f32[152,256]{1,0:T(8,128)S(1)} %get-tuple-element.15), channel_id=1, source_target_pairs={{0,2},{1,3},{2,0},{3,1},{4,6},{5,7},{6,4},{7,5},{8,10},{9,11},{10,... | collective-permute-start | bytes 466952 | tf_op jit(solution)/shard_map/ppermute | solution.py:492
  15.9 0.4 %own.1.refs_0_ = f32[152,256]{1,0:T(8,128)S(1)} custom-call(f32[4,2,24,256]{3,2,1,0:T(8,128)S(1)} %get-tuple-element.14.power_ref, f32[1032,256]{1,0:T(8,128)S(1)} %bank.1.refs_0_, f32[1032,256]{1,0:T(8,128)S(1)} %collective-permute-done.2.refs_1_), custom_call_target="tpu_custom_call" | custom-call | flops 1000000000 | bytes 1000000 | tf_op jit(solution)/shard_map/own/pallas_call | solution.py:495
  16.3 3.6 %collective-permute-done.3.refs_1_ = f32[152,256]{1,0:T(8,128)S(1)} collective-permute-done((f32[152,256]{1,0:T(8,128)S(1)}, f32[152,256]{1,0:T(8,128)S(1)}, u32[]{:S(2)}, u32[]{:S(2)}) %collective-permute-start.3) | collective-permute-done | bytes 155680 | tf_op jit(solution)/shard_map/ppermute | solution.py:492
  19.9 0.7 %final.1 = (f32[96,128]{1,0:T(8,128)}, f32[96,128]{1,0:T(8,128)}, f32[96,128]{1,0:T(8,128)}) custom-call(f32[152,256]{1,0:T(8,128)S(1)} %own.1.refs_0_, f32[152,256]{1,0:T(8,128)S(1)} %collective-permute-done.3.refs_1_), custom_call_target="tpu_custom_call" | custom-call | tf_op jit(solution)/shard_map/final/pallas_call | solution.py:504
  (2 shorter events, 0.0 us)
Async XLA Ops:
  1.8 1.0 %copy-start.5 = (f32[32768]{0:T(1024)S(1)}, f32[32768]{0:T(1024)}, u32[]{:S(2)}) copy-start(f32[32768]{0:T(1024)} %param.15) | copy-start | bytes 393220
  2.8 4.1 %copy-start = (bf16[3,512,256]{2,1,0:T(8,128)(2,1)S(1)}, bf16[3,512,256]{2,1,0:T(8,128)(2,1)}, u32[]{:S(2)}) copy-start(bf16[3,512,256]{2,1,0:T(8,128)(2,1)} %constant.14.clone.first_ref) | copy-start | bytes 2359300
  2.8 4.1 %copy-start.4 = (f32[49152]{0:T(1024)S(1)}, f32[49152]{0:T(1024)}, u32[]{:S(2)}) copy-start(f32[49152]{0:T(1024)} %param.14) | copy-start | bytes 589828
  2.8 7.6 %copy-start.3 = (bf16[512,384]{1,0:T(8,128)(2,1)S(1)}, bf16[512,384]{1,0:T(8,128)(2,1)}, u32[]{:S(2)}) copy-start(bf16[512,384]{1,0:T(8,128)(2,1)} %constant.15.clone.head_ref) | copy-start | bytes 1179652
  3.3 7.1 %copy-start.1 = (bf16[3,512,256]{2,1,0:T(8,128)(2,1)S(1)}, bf16[3,512,256]{2,1,0:T(8,128)(2,1)}, u32[]{:S(2)}) copy-start(bf16[3,512,256]{2,1,0:T(8,128)(2,1)} %constant.16.clone.second_ref) | copy-start | bytes 2359300
  3.3 7.1 %copy-start.2 = (f32[2,256,256]{2,1,0:T(8,128)S(1)}, f32[2,256,256]{2,1,0:T(8,128)}, u32[]{:S(2)}) copy-start(f32[2,256,256]{2,1,0:T(8,128)} %constant.19.clone.twist_ref.refs_4_) | copy-start | bytes 1572868
  3.3 8.3 %collective-permute-start.2 = (f32[1032,256]{1,0:T(8,128)S(1)}, f32[1032,256]{1,0:T(8,128)S(1)}, u32[]{:S(2)}, u32[]{:S(2)}) collective-permute-start(f32[1032,256]{1,0:T(8,128)S(1)} %bank.1.refs_0_), channel_id=1, source_target_pairs={{0,1},{1,0},{2,3},{3,2},{4,5},{5,4},{6,7},{7,6},{8,9},{9,8},{10,11... | collective-permute-start | bytes 3170312 | tf_op jit(solution)/shard_map/ppermute | solution.py:458
  3.9 3.6 %collective-permute-start.1 = (f32[128,128]{1,0:T(8,128)S(1)}, f32[128,128]{1,0:T(8,128)S(1)}, u32[]{:S(2)}, u32[]{:S(2)}) collective-permute-start(f32[128,128]{1,0:T(8,128)S(1)} %get-tuple-element.12), channel_id=1, source_target_pairs={{0,1},{1,0},{2,3},{3,2},{4,5},{5,4},{6,7},{7,6},{8,12},{9,13},{10,... | collective-permute-start | bytes 196616 | tf_op jit(solution)/shard_map/ppermute | solution.py:447
  4.0 6.5 %collective-permute-start = (f32[128,128]{1,0:T(8,128)S(1)}, f32[128,128]{1,0:T(8,128)S(1)}, u32[]{:S(2)}, u32[]{:S(2)}) collective-permute-start(f32[128,128]{1,0:T(8,128)S(1)} %get-tuple-element.12), channel_id=1, source_target_pairs={{0,4},{4,8},{8,0},{12,16},{16,20},{20,24},{24,28},{28,12},{1,5},{5... | collective-permute-start | bytes 196616 | tf_op jit(solution)/shard_map/ppermute | solution.py:445
  7.5 4.1 %copy-start.6 = (bf16[2,3,128,256]{3,2,1,0:T(8,128)(2,1)S(1)}, bf16[2,3,128,256]{3,2,1,0:T(8,128)(2,1)}, u32[]{:S(2)}) copy-start(bf16[2,3,128,256]{3,2,1,0:T(8,128)(2,1)} %constant.17.clone.refs_2_) | copy-start | bytes 1179652
  7.5 4.1 %copy-start.7 = (bf16[4,2,48,256]{3,2,1,0:T(8,128)(2,1)S(1)}, bf16[4,2,48,256]{3,2,1,0:T(8,128)(2,1)}, u32[]{:S(2)}) copy-start(bf16[4,2,48,256]{3,2,1,0:T(8,128)(2,1)} %constant.18.clone.refs_3_) | copy-start | bytes 589828
  7.5 4.1 %copy-start.8 = (f32[2,128,128]{2,1,0:T(8,128)S(1)}, f32[2,128,128]{2,1,0:T(8,128)}, u32[]{:S(2)}) copy-start(f32[2,128,128]{2,1,0:T(8,128)} %constant.20.clone.refs_5_) | copy-start | bytes 393220
  14.3 5.6 %collective-permute-start.3 = (f32[152,256]{1,0:T(8,128)S(1)}, f32[152,256]{1,0:T(8,128)S(1)}, u32[]{:S(2)}, u32[]{:S(2)}) collective-permute-start(f32[152,256]{1,0:T(8,128)S(1)} %get-tuple-element.15), channel_id=1, source_target_pairs={{0,2},{1,3},{2,0},{3,1},{4,6},{5,7},{6,4},{7,5},{8,10},{9,11},{10,... | collective-permute-start | bytes 466952 | tf_op jit(solution)/shard_map/ppermute | solution.py:492

commit v5 on v4

--- a/solution.py
+++ b/solution.py
@@ -20,6 +20,7 @@
 
 TERMS = ((0, 0), (0, 1), (1, 0), (1, 1), (0, 2), (2, 0))
 FEW = TERMS[:3]
+MOST = TERMS[:5]
 PARTS = 1 + max(max(term) for term in TERMS)
 
 
@@ -65,22 +66,21 @@
         parts = parts_of_table(complex_rows(angle, 1.0).T)
         third.append(np.stack(parts))
     own = hop_rows // parts_out // 2
-    fourth = []
+    fourth = np.zeros((parts_out, 2, 2, 2 * padded(own), FA), jnp.bfloat16)
     for dest in range(parts_out):
-        angle = (dest * own + np.arange(own))[:, None] * index[None, :HALF] % HALF * (2.0 * full)
-        block = complex_rows(angle, 1.0).reshape(2, own, FA)
-        block = np.pad(block, ((0, 0), (0, padded(own) - own), (0, 0))).reshape(-1, FA)
-        fourth.append(np.stack(parts_of_table(block)[:2]))
+        for odd in range(2):
+            row = 2 * (dest * own + np.arange(own)) + odd
+            block = complex_rows(row[:, None] * index[None, :HALF] % FA * full, 1.0).reshape(2, own, FA)
+            block = np.pad(block, ((0, 0), (0, padded(own) - own), (0, 0))).reshape(-1, FA)
+            fourth[dest, odd] = np.stack(parts_of_table(block)[:2])
     fine = grid * (2.0 * math.pi / NFFT)
-    turn = np.repeat(index[:HALF, None] * full, LANES, axis=1)
     return {
         "first": np.stack(first),
         "head": head,
         "second": second.reshape(PARTS, 2 * FA, FA),
         "third": np.stack(third),
-        "fourth": np.stack(fourth),
+        "fourth": fourth,
         "twist": np.stack([np.cos(fine), np.sin(fine)]).astype(np.float32),
-        "turn": np.stack([np.cos(turn), np.sin(turn)]).astype(np.float32),
     }
 
 
@@ -106,34 +106,35 @@
     return jnp.concatenate([parts[j] for _, j in terms], axis=0)
 
 
+SMALL = [1.0, 3.5156229, 3.0899424, 1.2067492, 0.2659732, 0.0360768, 0.0045813]
+LARGE = [
+    0.39894228,
+    0.01328592,
+    0.00225319,
+    -0.00157565,
+    0.00916281,
+    -0.02057706,
+    0.02635537,
+    -0.01647633,
+    0.00392377,
+]
+EDGE = 3.75
+
+
+def polynomial(coefficients, value):
+    total = coefficients[-1]
+    for coefficient in coefficients[-2::-1]:
+        total = coefficient + value * total
+    return total
+
+
 def log_bessel(power):
-    inv = lax.rsqrt(jnp.maximum(power, 1e-30))
+    inv = lax.rsqrt(power)
     rho = power * inv
-    small = rho < 3.75
-    t = jnp.minimum(power, 3.75 * 3.75) * (1.0 / (3.75 * 3.75))
-    small_poly = 1.0 + t * (
-        3.5156229
-        + t * (3.0899424 + t * (1.2067492 + t * (0.2659732 + t * (0.0360768 + t * 0.0045813))))
-    )
-    q = jnp.minimum(3.75 * inv, 1.0)
-    large_poly = 0.39894228 + q * (
-        0.01328592
-        + q
-        * (
-            0.00225319
-            + q
-            * (
-                -0.00157565
-                + q
-                * (
-                    0.00916281
-                    + q
-                    * (-0.02057706 + q * (0.02635537 + q * (-0.01647633 + q * 0.00392377)))
-                )
-            )
-        )
-    )
-    inner = jnp.where(small, small_poly, large_poly * lax.rsqrt(jnp.maximum(rho, 3.75)))
+    small = power < EDGE * EDGE
+    small_poly = polynomial([c / EDGE ** (2 * i) for i, c in enumerate(SMALL)], power)
+    large_poly = polynomial([c * EDGE**i for i, c in enumerate(LARGE)], inv)
+    inner = jnp.where(small, small_poly, large_poly * lax.rsqrt(rho))
     return jnp.where(small, 0.0, rho) + jnp.log(inner)
 
 
@@ -236,13 +237,22 @@
     if len(halos) > 1:
         halo = jnp.where(seg == segs // 2 - 1, frame_of(halos[1]), halo)
     halo = jnp.where(seg == 0, 0.0, halo)
-    section = section_ref[...] + dot(head_ref[...], right_terms(split(halo)))
-    re, im = section[:FA], section[FA:]
-    turn_cos, turn_sin = twist_ref[0], twist_ref[1]
-    turned = jnp.concatenate([re * turn_cos + im * turn_sin, im * turn_cos - re * turn_sin], axis=1)
-    spec = dot(left_terms(split(turned)), right_terms([second_ref[p] for p in range(PARTS)]))
-    spec_ref[0] = spec
-    spec_ref[1] = swapped(spec)
+    halo_terms = right_terms(split(halo))
+    second = right_terms([second_ref[p] for p in range(PARTS)])
+    size = FA // 2
+    sections = []
+    for r in range(0, FA, size):
+        both = jnp.concatenate([head_ref[r : r + size, :], head_ref[FA + r : FA + r + size, :]], axis=0)
+        sections.append(dot(both, halo_terms))
+    for i, extra in enumerate(sections):
+        here = slice(i * size, (i + 1) * size)
+        re = section_ref[here, :] + extra[:size]
+        im = section_ref[FA + i * size : FA + (i + 1) * size, :] + extra[size:]
+        turn_cos, turn_sin = twist_ref[0, here, :], twist_ref[1, here, :]
+        turned = jnp.concatenate([re * turn_cos + im * turn_sin, im * turn_cos - re * turn_sin], axis=1)
+        spec = dot(left_terms(split(turned)), second)
+        spec_ref[0, here, :] = spec
+        spec_ref[1, here, :] = swapped(spec)
 
 
 def swapped(value):
@@ -252,35 +262,47 @@
     )
 
 
-def powers_of(spec_ref, bank_ref, k, third_ref, left, twist_ref, turn_ref):
+ROWS = 32
+
+
+def product_terms(spec_ref, bank_ref, k):
     first = 2 * k * FA
-    prod = spec_ref[0] * bank_ref[first : first + FA, :] + spec_ref[1] * bank_ref[first + FA : first + 2 * FA, :]
-    even, odd = (
-        dot(
-            left_terms(split(prod[:, q * LANES : (q + 1) * LANES])),
-            right_terms([third_ref[q, p] for p in range(PARTS)]),
+    parts = [[], []]
+    for r in range(0, FA, ROWS):
+        here = slice(r, r + ROWS)
+        prod = (
+            spec_ref[0, here, :] * bank_ref[first + r : first + r + ROWS, :]
+            + spec_ref[1, here, :] * bank_ref[first + FA + r : first + FA + r + ROWS, :]
         )
+        for q in range(2):
+            parts[q].append(left_terms(split(prod[:, q * LANES : (q + 1) * LANES], 2), MOST))
+    return [jnp.concatenate(part, axis=0) for part in parts]
+
+
+def last_terms(even, odd, twist_ref):
+    parts = [[[], []] for _ in range(4)]
+    for r in range(0, HALF, ROWS):
+        turned = []
+        for here in (slice(r, r + ROWS), slice(HALF + r, HALF + r + ROWS)):
+            plus, minus = even[here] + odd[here], even[here] - odd[here]
+            in_re = jnp.concatenate([plus[:, :HALF], minus[:, :HALF]], axis=1)
+            in_im = jnp.concatenate([plus[:, HALF:], minus[:, HALF:]], axis=1)
+            turn_cos, turn_sin = twist_ref[0, here, :], twist_ref[1, here, :]
+            turned.append(
+                (in_re * turn_cos - in_im * turn_sin, in_re * turn_sin + in_im * turn_cos)
+            )
+        (low_re, low_im), (high_re, high_im) = turned
+        values = (low_re + high_re, low_im + high_im, low_re - high_re, low_im - high_im)
+        for part, value in zip(parts, values):
+            for p, piece in enumerate(split(value, 2)):
+                part[p].append(piece)
+    return [
+        right_terms([jnp.concatenate(parts[2 * q][p] + parts[2 * q + 1][p], axis=0) for p in range(2)], FEW)
         for q in range(2)
-    )
-    plus, minus = even + odd, even - odd
-    in_re = jnp.concatenate([plus[:, :HALF], minus[:, :HALF]], axis=1)
-    in_im = jnp.concatenate([plus[:, HALF:], minus[:, HALF:]], axis=1)
-    turn_cos, turn_sin = twist_ref[0], twist_ref[1]
-    out_re = in_re * turn_cos - in_im * turn_sin
-    out_im = in_re * turn_sin + in_im * turn_cos
-    sum_re, sum_im = out_re[:HALF] + out_re[HALF:], out_im[:HALF] + out_im[HALF:]
-    gap_re, gap_im = out_re[:HALF] - out_re[HALF:], out_im[:HALF] - out_im[HALF:]
-    half_cos = jnp.concatenate([turn_ref[0]] * 2, axis=1)
-    half_sin = jnp.concatenate([turn_ref[1]] * 2, axis=1)
-    odd_re, odd_im = gap_re * half_cos - gap_im * half_sin, gap_re * half_sin + gap_im * half_cos
-    return [
-        dot(left, right_terms(split(jnp.concatenate(piece, axis=0), 2), FEW))
-        for piece in ((sum_re, sum_im), (odd_re, odd_im))
     ]
 
 
-def marginal(powers, traits):
-    scores = [log_bessel(power) for power in powers]
+def marginal(scores, traits):
     peak = functools.reduce(jnp.maximum, scores)
     masses = [weight * jnp.exp(score - peak) for score, (weight, _, _) in zip(scores, traits)]
     total = functools.reduce(jnp.add, masses)
@@ -298,10 +320,10 @@
     ]
 
 
-def store_marginal(out_ref, powers, traits):
-    rows = powers[0][0].shape[0]
+def store_marginal(out_ref, scores, traits):
+    rows = scores[0][0].shape[0]
     for q in range(2):
-        for i, value in enumerate(marginal([power[q] for power in powers], traits)):
+        for i, value in enumerate(marginal([score[q] for score in scores], traits)):
             first = (3 * q + i) * rows
             out_ref[first : first + rows, :] = value
     prior = functools.reduce(jnp.add, [trait[0] for trait in traits])
@@ -328,37 +350,48 @@
 
 
 def main_kernel(spec_ref, *refs, group):
-    banks, (third_ref, fourth_ref, twist_ref, turn_ref, own_ref, *outs) = refs[:group], refs[group:]
+    banks, (third_ref, fourth_ref, twist_ref, own_ref, *outs) = refs[:group], refs[group:]
     n = fourth_ref.shape[0]
     count = (banks[0].shape[0] - trait_rows(1)) // (2 * FA)
     me = lax.axis_index("bank")
     dests = [partner(me, r, n, group) for r in range(n // group)]
-    block = fourth_ref.shape[2]
-    left = left_terms(
-        [jnp.concatenate([fourth_ref[dest, p] for dest in dests], axis=0) for p in range(2)], FEW
-    )
-    powers = []
-    for bank in banks:
-        for k in range(count):
-            powers.append([])
-            for corr in powers_of(spec_ref, bank, k, third_ref, left, twist_ref, turn_ref):
-                powers[-1].append([])
-                for r in range(len(dests)):
-                    re = corr[r * block : r * block + block // 2]
-                    im = corr[r * block + block // 2 : (r + 1) * block]
-                    powers[-1][-1].append(re * re + im * im)
+    block = fourth_ref.shape[3]
+    lefts = [
+        left_terms(
+            [jnp.concatenate([fourth_ref[dest, q, p] for dest in dests], axis=0) for p in range(2)], FEW
+        )
+        for q in range(2)
+    ]
+    third = [right_terms([third_ref[q, p] for p in range(PARTS)], MOST) for q in range(2)]
+    work = [(bank, k) for bank in banks for k in range(count)]
+
+    def sums(bank, k):
+        terms = product_terms(spec_ref, bank, k)
+        return [dot(terms[q], third[q]) for q in range(2)]
+
+    scores = []
+    ready = sums(*work[0])
+    for i in range(len(work)):
+        now, ready = ready, sums(*work[i + 1]) if i + 1 < len(work) else None
+        scores.append([[] for _ in outs])
+        for q, piece in enumerate(last_terms(*now, twist_ref)):
+            corr = dot(lefts[q], piece)
+            for r in range(len(dests)):
+                re = corr[r * block : r * block + block // 2]
+                im = corr[r * block + block // 2 : (r + 1) * block]
+                if r:
+                    scores[i][r - 1].append(log_bessel(re * re + im * im))
+                else:
+                    own_ref[i, q] = re * re + im * im
     traits = traits_of(banks, count)
-    for r, out in enumerate(outs, 1):
-        store_marginal(out, [[power[q][r] for q in range(2)] for power in powers], traits)
-    for i, power in enumerate(powers):
-        for q in range(2):
-            own_ref[i, q] = power[q][0]
+    for r, out in enumerate(outs):
+        store_marginal(out, [score[r] for score in scores], traits)
 
 
 def own_kernel(power_ref, *refs):
     *banks, out_ref = refs
-    powers = [[power_ref[i, q] for q in range(2)] for i in range(power_ref.shape[0])]
-    store_marginal(out_ref, powers, traits_of(banks, power_ref.shape[0] // len(banks)))
+    scores = [[log_bessel(power_ref[i, q]) for q in range(2)] for i in range(power_ref.shape[0])]
+    store_marginal(out_ref, scores, traits_of(banks, power_ref.shape[0] // len(banks)))
 
 
 def final_kernel(*refs):
@@ -481,13 +514,13 @@
     side = pltpu.VMEM((6 * own_rows + 8, FA), F32)
     powers, *outs = pl.pallas_call(
         functools.partial(main_kernel, group=group),
-        in_specs=[VMEM] * (5 + group),
+        in_specs=[VMEM] * (4 + group),
         out_specs=[VMEM] * (n // group),
         out_shape=[pltpu.VMEM((count * group, 2, own_rows, FA), F32)] + [side] * (n // group - 1),
         compiler_params=params(20),
         cost_estimate=pl.CostEstimate(flops=4 * 10**9, bytes_accessed=4 * 10**6, transcendentals=0),
         name="main",
-    )(spec, *banks, *(table[key] for key in ("third", "fourth", "twist", "turn")))
+    )(spec, *banks, *(table[key] for key in ("third", "fourth", "twist")))
     sides = [
         lax.ppermute(out, "bank", [(i, partner(i, r, n, group)) for i in range(n)])
         for r, out in enumerate(outs, 1)

time: 20.8 us -> 19.9 us (0.957)
  Pallas kernels: 6.98 us -> 6.14 us
    pallas_call x1, Pallas kernels: 2.66 us -> 1.97 us  [steps(): pl.pallas_call(functools.partial(main_kernel, group=group), in_specs=[VME...]
where the time goes in v5:
time: 19.9 us; the launch traced here: 19.8 us
  waiting for transfers between devices  6.56 us (33%)
  Pallas kernels  6.14 us (31%)
  starting transfers between devices  5.12 us (26%)
  local copies, waits for them, and re-layouts  1.18 us (6%)
  between operations  0.78 us (4%)
    ppermute x1, waiting for transfers between devices, steps(): lax.ppermute(out, 'bank', [(i, partner(i, r, n, group)) for i in range(n)])  3.65 us
    ppermute x1, starting transfers between devices, steps(): halos = [lax.ppermute(tail, 'seg', ring)]  2.91 us
    ppermute x1, waiting for transfers between devices, steps(): halos = [lax.ppermute(tail, 'seg', ring)]  2.9 us
    pallas_call x1, Pallas kernels, steps(): pl.pallas_call(functools.partial(main_kernel, group=group), in_specs=[VME...  1.97 us
    ppermute x1, starting transfers between devices, steps(): lax.ppermute(out, 'bank', [(i, partner(i, r, n, group)) for i in range(n)])  1.58 us
    reshape x1, local copies, waits for them, and re-layouts, steps(): templates.astype(F32).reshape(2, count, -1, LANES)  1.12 us
    pallas_call x1, Pallas kernels, steps(): pl.pallas_call(functools.partial(spectrum_kernel, segs=segs), in_specs=[V...  1.07 us
    pallas_call x1, Pallas kernels, steps(): pl.pallas_call(tail_kernel, in_specs=[HBM] * 5, out_specs=[VMEM] * 3, out...  0.99 us
  transfers between devices with their start and end apart: 4, of which 2 were waited for; matrix products, arithmetic and copies ran while one was open for 0% of the time, Pallas kernels for 10%

profile of v5, /device:TPU:0, one launch (start us, length us, event | category | flops | bytes accessed | tf_op | source)
XLA Modules:
  0.0 19.8 jit_solution(4086841753655247873)
XLA Ops:
  0.6 1.1 %reshape.34.tmpl_ref = f32[2,2,256,128]{3,2,1,0:T(8,128)S(1)} reshape(bf16[2,2,32768]{2,1,0:T(2,128)(2,1)} %param.15) | data formatting | bytes 786432 | tf_op jit(solution)/shard_map/reshape | solution.py:489
  1.8 0.0 copy-start.5
  1.8 1.0 %tail.1 = (f32[128,128]{1,0:T(8,128)S(1)}, f32[8,256]{1,0:T(8,128)S(1)}, f32[48,128]{1,0:T(8,128)S(1)}) custom-call(s32[2]{0:T(128)} %len_hbm.1, f32[2]{0:T(128)} %weight_hbm.1, f32[2]{0:T(128)} %chirp_hbm.1, s32[48]{0:T(128)} %valid_hbm.1, f32[384,128]{1,0:T(8,128)} %bitcast.5), custom_call_target="tpu_custom_call" | custom-call | flops 4000000000 | bytes 100000 | tf_op jit(solution)/shard_map/tail/pallas_call | solution.py:456
  2.8 0.0 copy-start
  2.8 0.0 copy-start.4
  2.8 0.0 copy-done.5
  2.8 0.0 copy-start.3
  2.8 0.5 %bank.1.refs_0_ = f32[1032,256]{1,0:T(8,128)S(1)} custom-call(f32[8,256]{1,0:T(8,128)S(1)} %get-tuple-element.13.traits_ref, f32[256,128]{1,0:T(8,128)S(1)} %bitcast.7, f32[2,2,256,128]{3,2,1,0:T(8,128)S(1)} %reshape.34.tmpl_ref), custom_call_target="tpu_custom_call" | custom-call | flops 1000000 | bytes 10000 | tf_op jit(solution)/shard_map/bank/pallas_call | solution.py:481
  3.3 0.0 copy-start.1
  3.3 0.0 copy-start.2
  3.3 0.6 %collective-permute-start.2 = (f32[1032,256]{1,0:T(8,128)S(1)}, f32[1032,256]{1,0:T(8,128)S(1)}, u32[]{:S(2)}, u32[]{:S(2)}) collective-permute-start(f32[1032,256]{1,0:T(8,128)S(1)} %bank.1.refs_0_), channel_id=1, source_target_pairs={{0,1},{1,0},{2,3},{3,2},{4,5},{5,4},{6,7},{7,6},{8,9},{9,8},{10,11... | collective-permute-start | bytes 3170312 | tf_op jit(solution)/shard_map/ppermute | solution.py:491
  3.9 0.1 collective-permute-start.1
  4.0 2.9 %collective-permute-start = (f32[128,128]{1,0:T(8,128)S(1)}, f32[128,128]{1,0:T(8,128)S(1)}, u32[]{:S(2)}, u32[]{:S(2)}) collective-permute-start(f32[128,128]{1,0:T(8,128)S(1)} %get-tuple-element.12), channel_id=1, source_target_pairs={{0,4},{4,8},{8,0},{12,16},{16,20},{20,24},{24,28},{28,12},{1,5},{5... | collective-permute-start | bytes 196616 | tf_op jit(solution)/shard_map/ppermute | solution.py:478
  6.9 0.0 copy-done
  6.9 0.0 copy-done.4
  6.9 0.6 %section.1.section_ref = f32[512,256]{1,0:T(8,128)S(1)} custom-call(f32[48,128]{1,0:T(8,128)S(1)} %get-tuple-element.11.gates_ref, f32[384,128]{1,0:T(8,128)S(1)} %bitcast.6, bf16[3,512,256]{2,1,0:T(8,128)(2,1)S(1)} %copy-done), custom_call_target="tpu_custom_call" | custom-call | flops 1000000 | bytes 10000 | tf_op jit(solution)/shard_map/section/pallas_call | solution.py:494
  7.5 0.0 copy-start.6
  7.5 0.0 copy-start.7
  7.5 0.0 collective-permute-done.1.refs_1_
  7.5 2.9 %collective-permute-done.refs_0_ = f32[128,128]{1,0:T(8,128)S(1)} collective-permute-done((f32[128,128]{1,0:T(8,128)S(1)}, f32[128,128]{1,0:T(8,128)S(1)}, u32[]{:S(2)}, u32[]{:S(2)}) %collective-permute-start) | collective-permute-done | bytes 65568 | tf_op jit(solution)/shard_map/ppermute | solution.py:478
  10.4 0.0 copy-done.3
  10.4 0.0 copy-done.1
  10.4 0.0 copy-done.2
  10.4 1.1 %spectrum.1.spec_ref = f32[2,256,256]{2,1,0:T(8,128)S(1)} custom-call(f32[512,256]{1,0:T(8,128)S(1)} %section.1.section_ref, bf16[512,384]{1,0:T(8,128)(2,1)S(1)} %copy-done.3, bf16[3,512,256]{2,1,0:T(8,128)(2,1)S(1)} %copy-done.1, f32[2,256,256]{2,1,0:T(8,128)S(1)} %copy-done.2, f32[128,128]{1,0:T(8,128)S(1)} %collective-permute-done.refs_0_, ...), custom_call_target="tpu_custom_call" | custom-call | flops 1000000 | bytes 10000 | tf_op jit(solution)/shard_map/spectrum/pallas_call | solution.py:504
  11.5 0.0 collective-permute-done.2.refs_1_
  11.5 0.0 copy-done.6
  11.5 0.0 copy-done.7
  11.5 2.0 %main.1 = (f32[4,2,24,256]{3,2,1,0:T(8,128)S(1)}, f32[152,256]{1,0:T(8,128)S(1)}) custom-call(f32[2,256,256]{2,1,0:T(8,128)S(1)} %spectrum.1.spec_ref, f32[1032,256]{1,0:T(8,128)S(1)} %bank.1.refs_0_, f32[1032,256]{1,0:T(8,128)S(1)} %collective-permute-done.2.refs_1_, bf16[2,3,128,256]{3,2,1,0:T(8,128)(2,1)S(1)} %copy-done.7, ...), custom_call_target="tpu_custom_call" | custom-call | flops 4000000000 | bytes 4000000 | tf_op jit(solution)/shard_map/main/pallas_call | solution.py:515
  13.5 1.6 %collective-permute-start.3 = (f32[152,256]{1,0:T(8,128)S(1)}, f32[152,256]{1,0:T(8,128)S(1)}, u32[]{:S(2)}, u32[]{:S(2)}) collective-permute-start(f32[152,256]{1,0:T(8,128)S(1)} %get-tuple-element.15), channel_id=1, source_target_pairs={{0,2},{1,3},{2,0},{3,1},{4,6},{5,7},{6,4},{7,5},{8,10},{9,11},{10,... | collective-permute-start | bytes 466952 | tf_op jit(solution)/shard_map/ppermute | solution.py:525
  15.1 0.3 %own.1.refs_0_ = f32[152,256]{1,0:T(8,128)S(1)} custom-call(f32[4,2,24,256]{3,2,1,0:T(8,128)S(1)} %get-tuple-element.14.power_ref, f32[1032,256]{1,0:T(8,128)S(1)} %bank.1.refs_0_, f32[1032,256]{1,0:T(8,128)S(1)} %collective-permute-done.2.refs_1_), custom_call_target="tpu_custom_call" | custom-call | flops 1000000000 | bytes 1000000 | tf_op jit(solution)/shard_map/own/pallas_call | solution.py:528
  15.4 3.7 %collective-permute-done.3.refs_1_ = f32[152,256]{1,0:T(8,128)S(1)} collective-permute-done((f32[152,256]{1,0:T(8,128)S(1)}, f32[152,256]{1,0:T(8,128)S(1)}, u32[]{:S(2)}, u32[]{:S(2)}) %collective-permute-start.3) | collective-permute-done | bytes 155680 | tf_op jit(solution)/shard_map/ppermute | solution.py:525
  19.1 0.7 %final.1 = (f32[96,128]{1,0:T(8,128)}, f32[96,128]{1,0:T(8,128)}, f32[96,128]{1,0:T(8,128)}) custom-call(f32[152,256]{1,0:T(8,128)S(1)} %own.1.refs_0_, f32[152,256]{1,0:T(8,128)S(1)} %collective-permute-done.3.refs_1_), custom_call_target="tpu_custom_call" | custom-call | tf_op jit(solution)/shard_map/final/pallas_call | solution.py:537
Async XLA Ops:
  1.8 1.0 %copy-start.5 = (f32[32768]{0:T(1024)S(1)}, f32[32768]{0:T(1024)}, u32[]{:S(2)}) copy-start(f32[32768]{0:T(1024)} %param.14) | copy-start | bytes 393220
  2.8 4.1 %copy-start = (bf16[3,512,256]{2,1,0:T(8,128)(2,1)S(1)}, bf16[3,512,256]{2,1,0:T(8,128)(2,1)}, u32[]{:S(2)}) copy-start(bf16[3,512,256]{2,1,0:T(8,128)(2,1)} %constant.12.clone.first_ref) | copy-start | bytes 2359300
  2.8 4.1 %copy-start.4 = (f32[49152]{0:T(1024)S(1)}, f32[49152]{0:T(1024)}, u32[]{:S(2)}) copy-start(f32[49152]{0:T(1024)} %param.13) | copy-start | bytes 589828
  2.8 7.6 %copy-start.3 = (bf16[512,384]{1,0:T(8,128)(2,1)S(1)}, bf16[512,384]{1,0:T(8,128)(2,1)}, u32[]{:S(2)}) copy-start(bf16[512,384]{1,0:T(8,128)(2,1)} %constant.13.clone.head_ref) | copy-start | bytes 1179652
  3.3 7.1 %copy-start.1 = (bf16[3,512,256]{2,1,0:T(8,128)(2,1)S(1)}, bf16[3,512,256]{2,1,0:T(8,128)(2,1)}, u32[]{:S(2)}) copy-start(bf16[3,512,256]{2,1,0:T(8,128)(2,1)} %constant.14.clone.second_ref) | copy-start | bytes 2359300
  3.3 7.1 %copy-start.2 = (f32[2,256,256]{2,1,0:T(8,128)S(1)}, f32[2,256,256]{2,1,0:T(8,128)}, u32[]{:S(2)}) copy-start(f32[2,256,256]{2,1,0:T(8,128)} %constant.17.clone.twist_ref.refs_4_) | copy-start | bytes 1572868
  3.3 8.2 %collective-permute-start.2 = (f32[1032,256]{1,0:T(8,128)S(1)}, f32[1032,256]{1,0:T(8,128)S(1)}, u32[]{:S(2)}, u32[]{:S(2)}) collective-permute-start(f32[1032,256]{1,0:T(8,128)S(1)} %bank.1.refs_0_), channel_id=1, source_target_pairs={{0,1},{1,0},{2,3},{3,2},{4,5},{5,4},{6,7},{7,6},{8,9},{9,8},{10,11... | collective-permute-start | bytes 3170312 | tf_op jit(solution)/shard_map/ppermute | solution.py:491
  3.9 3.6 %collective-permute-start.1 = (f32[128,128]{1,0:T(8,128)S(1)}, f32[128,128]{1,0:T(8,128)S(1)}, u32[]{:S(2)}, u32[]{:S(2)}) collective-permute-start(f32[128,128]{1,0:T(8,128)S(1)} %get-tuple-element.12), channel_id=1, source_target_pairs={{0,1},{1,0},{2,3},{3,2},{4,5},{5,4},{6,7},{7,6},{8,12},{9,13},{10,... | collective-permute-start | bytes 196616 | tf_op jit(solution)/shard_map/ppermute | solution.py:480
  4.0 6.5 %collective-permute-start = (f32[128,128]{1,0:T(8,128)S(1)}, f32[128,128]{1,0:T(8,128)S(1)}, u32[]{:S(2)}, u32[]{:S(2)}) collective-permute-start(f32[128,128]{1,0:T(8,128)S(1)} %get-tuple-element.12), channel_id=1, source_target_pairs={{0,4},{4,8},{8,0},{12,16},{16,20},{20,24},{24,28},{28,12},{1,5},{5... | collective-permute-start | bytes 196616 | tf_op jit(solution)/shard_map/ppermute | solution.py:478
  7.5 4.0 %copy-start.6 = (bf16[4,2,2,48,256]{4,3,2,1,0:T(8,128)(2,1)S(1)}, bf16[4,2,2,48,256]{4,3,2,1,0:T(8,128)(2,1)}, u32[]{:S(2)}) copy-start(bf16[4,2,2,48,256]{4,3,2,1,0:T(8,128)(2,1)} %constant.16.clone.refs_3_) | copy-start | bytes 1179652
  7.5 4.0 %copy-start.7 = (bf16[2,3,128,256]{3,2,1,0:T(8,128)(2,1)S(1)}, bf16[2,3,128,256]{3,2,1,0:T(8,128)(2,1)}, u32[]{:S(2)}) copy-start(bf16[2,3,128,256]{3,2,1,0:T(8,128)(2,1)} %constant.15.clone.refs_2_) | copy-start | bytes 1179652
  13.5 5.6 %collective-permute-start.3 = (f32[152,256]{1,0:T(8,128)S(1)}, f32[152,256]{1,0:T(8,128)S(1)}, u32[]{:S(2)}, u32[]{:S(2)}) collective-permute-start(f32[152,256]{1,0:T(8,128)S(1)} %get-tuple-element.15), channel_id=1, source_target_pairs={{0,2},{1,3},{2,0},{3,1},{4,6},{5,7},{6,4},{7,5},{8,10},{9,11},{10,... | collective-permute-start | bytes 466952 | tf_op jit(solution)/shard_map/ppermute | solution.py:525
